TPU v7x, 32 devices: a whole 2x2x4 slice. The times are simulated.
32 devices in a mesh: dp: 8 (over y, x, core), tensor: 4 (over z).
Axes of the slice: x: 2, y: 2, z: 4, core: 2. Of those that a mesh axis runs over, the one named last changes fastest.
Arguments:
- tokens: bfloat16 [2, 8192, 768], P(None, ('dp', 'tensor')), may hold values from -6 to 6
- cotangent: bfloat16 [2, 8192, 768], P(None, ('dp', 'tensor')), may hold values from -6 to 6
- lengths: int32 [2, 8, 4], P(None, 'dp'), may hold values from 1 to 900, 1024 in all within a row
- padding: int32 [2, 8192], P(None, 'dp'), may hold values 0 or 1
- ln_gain: bfloat16 [1, 2, 768], P(None, None, 'dp'), may hold values from 0.5 to 1.5
- w_qkv: bfloat16 [1, 768, 3, 768], P(None, 'dp', None, 'tensor'), may hold values from -0.3125 to 0.3125
- w_out: bfloat16 [1, 768, 768], P(None, 'tensor', 'dp'), may hold values from -0.875 to 0.875
- w_up: bfloat16 [1, 768, 3072], P(None, 'dp', 'tensor'), may hold values from -0.21875 to 0.21875
- w_down: bfloat16 [1, 3072, 768], P(None, 'tensor', 'dp'), may hold values from -0.109375 to 0.109375
Outputs:
- layer_out: float32 [2, 8192, 768], P(None, ('dp', 'tensor'))
- input_grad: float32 [2, 8192, 768], P(None, ('dp', 'tensor'))
- gain_grad: float32 [1536], P(('dp', 'tensor'))
- qkv_grad: float32 [1, 768, 3, 768], P(None, 'dp', None, 'tensor')
- out_grad: float32 [1, 768, 768], P(None, 'tensor', 'dp')
- up_grad: float32 [1, 768, 3072], P(None, 'dp', 'tensor')
- down_grad: float32 [1, 3072, 768], P(None, 'tensor', 'dp')
Inputs may be any that keep to these rules, and one draw needn't show every extreme that they name: In every block the 4 image lengths sum to 1024, and one image has exactly 900 tokens.
All inputs are finite; a program needn't handle non-finite values. No bound on the sum of `padding` on one device may be relied on, other than what follows from the above.
Results may differ from a plain program's by a relative error of at most 0.012.
The roundings to bfloat16 on the way count: a program that leaves them out, or rounds other values in their place, can miss the bound.
Values may be sent and summed in bfloat16 or wider, within the bound.
A program may use at most 128 MiB of HBM per device.

v0:
```python
import jax
import jax.numpy as jnp
from jax import lax
from jax.sharding import PartitionSpec as P

D = 768
HD = 64


NEGATIVE = -1e30
EPSILON = 1e-06


def normalize(row_block):
    average = jnp.mean(row_block, axis=-1, keepdims=True)
    centred = row_block - average
    variance = jnp.mean(centred * centred, axis=-1, keepdims=True)
    inverse = lax.rsqrt(variance + EPSILON)
    return (centred * inverse, inverse)


def norm_back(grad_out, gain_row, normed, inverse):
    scaled = grad_out * gain_row
    mean_grad = jnp.mean(scaled, axis=-1, keepdims=True)
    second = jnp.mean(scaled * normed, axis=-1, keepdims=True)
    return inverse * (scaled - mean_grad - normed * second)


def visible(lengths_row, padding_row):
    places = lax.iota(jnp.int32, padding_row.shape[0])
    bounds = jnp.cumsum(lengths_row)
    picture = jnp.sum((places[:, None] >= bounds[None, :]).astype(jnp.int32), axis=1)
    same_image = picture[:, None] == picture[None, :]
    return same_image & ((padding_row[None, :] == 1) | (places[:, None] == places[None, :]))


def gelu_exact(pre_values):
    return jax.nn.gelu(pre_values, approximate=False)


def masked_scores(queries, key_rows, allowed):
    scaling = queries.shape[-1] ** (-0.5)
    scores = (
        jnp.einsum("qhd,khd->hqk", queries, key_rows, preferred_element_type=jnp.float32) * scaling
    )
    return (jnp.where(allowed[None], scores, NEGATIVE), scaling)


def attend(stacked, allowed):
    scores, scaling = masked_scores(stacked[:, 0], stacked[:, 1], allowed)
    highest = jnp.max(scores, axis=-1, keepdims=True)
    exponent = jnp.exp(scores - highest)
    totals = jnp.sum(exponent, axis=-1, keepdims=True)
    rounded = (exponent / totals).astype(jnp.bfloat16)
    mixture = jnp.einsum("hqk,khd->qhd", rounded, stacked[:, 2], preferred_element_type=jnp.float32)
    return (mixture, highest, totals)


def attend_back(stacked, allowed, highest, totals, grad_mix):
    queries, key_rows, value_rows = (stacked[:, 0], stacked[:, 1], stacked[:, 2])
    scores, scaling = masked_scores(queries, key_rows, allowed)
    probability = jnp.exp(scores - highest) / totals
    rounded = probability.astype(jnp.bfloat16)
    grad_prob = jnp.einsum("qhd,khd->hqk", grad_mix, value_rows, preferred_element_type=jnp.float32)
    grad_values = jnp.einsum("hqk,qhd->khd", rounded, grad_mix, preferred_element_type=jnp.float32)
    inner_sum = jnp.sum(probability * grad_prob, axis=-1, keepdims=True)
    grad_scores = (probability * (grad_prob - inner_sum)).astype(jnp.bfloat16)
    grad_queries = (
        jnp.einsum("hqk,khd->qhd", grad_scores, key_rows, preferred_element_type=jnp.float32)
        * scaling
    )
    grad_keys = (
        jnp.einsum("hqk,qhd->khd", grad_scores, queries, preferred_element_type=jnp.float32)
        * scaling
    )
    return jnp.stack([grad_queries, grad_keys, grad_values], axis=1).astype(jnp.bfloat16)


def collect_weights(ln_gain, w_qkv, w_out, w_up, w_down, layer_index):
    return (
        lax.all_gather(ln_gain[layer_index], "dp", axis=1, tiled=True),
        lax.all_gather(w_qkv[layer_index], "dp", axis=0, tiled=True),
        lax.all_gather(w_out[layer_index], "dp", axis=1, tiled=True),
        lax.all_gather(w_up[layer_index], "dp", axis=0, tiled=True),
        lax.all_gather(w_down[layer_index], "dp", axis=1, tiled=True),
    )


def spread(block_rows):
    return lax.all_gather(block_rows, "tensor", axis=0, tiled=True)


def spread_grad(block_rows):
    return lax.all_gather(block_rows, "tensor", axis=0, tiled=True)


def collect_rows(operand, weight):
    return lax.psum_scatter(
        jnp.dot(operand, weight, preferred_element_type=jnp.float32),
        "tensor",
        scatter_dimension=0,
        tiled=True,
    )


def return_rows(operand, weight):
    return lax.psum_scatter(
        lax.dot_general(
            operand, weight, (((1,), (1,)), ((), ())), preferred_element_type=jnp.float32
        ),
        "tensor",
        scatter_dimension=0,
        tiled=True,
    )


def reduce_grads(pieces):
    return (
        lax.psum_scatter(pieces[0], "dp", scatter_dimension=0, tiled=True),
        lax.psum_scatter(pieces[1], "dp", scatter_dimension=1, tiled=True),
        lax.psum_scatter(pieces[2], "dp", scatter_dimension=0, tiled=True),
        lax.psum_scatter(pieces[3], "dp", scatter_dimension=1, tiled=True),
    )


def body(tokens, cotangent, lengths, padding, ln_gain, w_qkv, w_out, w_up, w_down):
    layer_count = w_qkv.shape[0]
    micro_count = tokens.shape[0]
    residual = [tokens[batch_index].astype(jnp.float32) for batch_index in range(micro_count)]
    visibility = [
        visible(lengths[batch_index, 0], padding[batch_index]) for batch_index in range(micro_count)
    ]
    saved = []
    stored_weights = []
    layer_index = 0
    stored_weights.append(None)
    for batch_index in range(micro_count):
        weights = collect_weights(ln_gain, w_qkv, w_out, w_up, w_down, layer_index)
        gain_pair, qkv_weight, out_weight, up_weight, down_weight = weights
        gain_first = gain_pair[0].astype(jnp.float32)
        gain_second = gain_pair[1].astype(jnp.float32)
        entering = residual[batch_index]
        normed, inverse = normalize(entering)
        first_input = spread((normed * gain_first).astype(jnp.bfloat16))
        triple = jnp.einsum(
            "rd,dcn->rcn", first_input, qkv_weight, preferred_element_type=jnp.float32
        ).astype(jnp.bfloat16)
        stacked = triple.reshape(triple.shape[0], 3, -1, HD)
        mixture, highest, totals = attend(stacked, visibility[batch_index])
        mix_rounded = mixture.reshape(mixture.shape[0], -1).astype(jnp.bfloat16)
        middle = entering + collect_rows(mix_rounded, out_weight)
        normed_two, inverse_two = normalize(middle)
        second_input = spread((normed_two * gain_second).astype(jnp.bfloat16))
        hidden_pre = jnp.dot(second_input, up_weight, preferred_element_type=jnp.float32)
        activated = gelu_exact(hidden_pre).astype(jnp.bfloat16)
        residual[batch_index] = middle + collect_rows(activated, down_weight)
        saved.append(
            (
                entering,
                first_input,
                stacked,
                highest,
                totals,
                mix_rounded,
                middle,
                second_input,
                hidden_pre,
                activated,
            )
        )
    gradients = [cotangent[batch_index].astype(jnp.float32) for batch_index in range(micro_count)]
    gain_parts = [jnp.zeros((2, D), jnp.float32)]
    weight_results = [None]
    for layer_index in reversed(range(layer_count)):
        summed = None
        for batch_index in range(micro_count):
            weights = collect_weights(ln_gain, w_qkv, w_out, w_up, w_down, layer_index)
            gain_pair, qkv_weight, out_weight, up_weight, down_weight = weights
            gain_first = gain_pair[0].astype(jnp.float32)
            gain_second = gain_pair[1].astype(jnp.float32)
            (
                entering,
                first_input,
                stacked,
                highest,
                totals,
                mix_rounded,
                middle,
                second_input,
                hidden_pre,
                activated,
            ) = saved[layer_index * micro_count + batch_index]
            incoming = gradients[batch_index]
            grad_down = spread_grad(incoming.astype(jnp.bfloat16))
            down_part = jnp.einsum(
                "rf,rd->fd", activated, grad_down, preferred_element_type=jnp.float32
            )
            grad_act = lax.dot_general(
                grad_down, down_weight, (((1,), (1,)), ((), ())), preferred_element_type=jnp.float32
            )
            pulled = jax.vjp(gelu_exact, hidden_pre)
            grad_pre = pulled[1](grad_act)[0].astype(jnp.bfloat16)
            up_part = jnp.einsum(
                "rd,rf->df", second_input, grad_pre, preferred_element_type=jnp.float32
            )
            grad_norm_two = return_rows(grad_pre, up_weight)
            normed_two, inverse_two = normalize(middle)
            gain_two_part = jnp.sum(grad_norm_two * normed_two, axis=0)
            incoming = incoming + norm_back(grad_norm_two, gain_second, normed_two, inverse_two)
            grad_branch = spread_grad(incoming.astype(jnp.bfloat16))
            out_part = jnp.einsum(
                "rk,rd->kd", mix_rounded, grad_branch, preferred_element_type=jnp.float32
            )
            grad_mix = lax.dot_general(
                grad_branch,
                out_weight,
                (((1,), (1,)), ((), ())),
                preferred_element_type=jnp.float32,
            )
            grad_mix = grad_mix.astype(jnp.bfloat16).reshape(grad_mix.shape[0], -1, HD)
            grad_triple = attend_back(stacked, visibility[batch_index], highest, totals, grad_mix)
            flat_triple = grad_triple.reshape(grad_triple.shape[0], 3, -1)
            qkv_part = jnp.einsum(
                "rd,rcn->dcn", first_input, flat_triple, preferred_element_type=jnp.float32
            )
            grad_norm_one = return_rows(
                flat_triple.reshape(flat_triple.shape[0], -1),
                qkv_weight.reshape(qkv_weight.shape[0], -1),
            )
            normed, inverse = normalize(entering)
            gain_one_part = jnp.sum(grad_norm_one * normed, axis=0)
            incoming = incoming + norm_back(grad_norm_one, gain_first, normed, inverse)
            gradients[batch_index] = incoming
            gain_parts[layer_index] = gain_parts[layer_index] + jnp.stack(
                [gain_one_part, gain_two_part]
            )
            pieces = (qkv_part, out_part, up_part, down_part)
            if summed is None:
                summed = pieces
            else:
                summed = tuple((older + newer for older, newer in zip(summed, pieces)))
        summed = reduce_grads(summed)
        weight_results[layer_index] = summed
    gain_flat = jnp.stack(gain_parts).reshape(-1)
    gain_result = lax.psum_scatter(gain_flat, ("dp", "tensor"), scatter_dimension=0, tiled=True)
    layer_out = jnp.stack(residual)
    input_grad = jnp.stack(gradients)
    qkv_grad = jnp.stack([weight_results[0][0]])
    out_grad = jnp.stack([weight_results[0][1]])
    up_grad = jnp.stack([weight_results[0][2]])
    down_grad = jnp.stack([weight_results[0][3]])
    return (layer_out, input_grad, gain_result, qkv_grad, out_grad, up_grad, down_grad)


def solution(mesh):
    return jax.shard_map(
        body,
        mesh=mesh,
        in_specs=(
            P(None, ("dp", "tensor"), None),
            P(None, ("dp", "tensor"), None),
            P(None, "dp", None),
            P(None, "dp"),
            P(None, None, "dp"),
            P(None, "dp", None, "tensor"),
            P(None, "tensor", "dp"),
            P(None, "dp", "tensor"),
            P(None, "tensor", "dp"),
        ),
        out_specs=(
            P(None, ("dp", "tensor"), None),
            P(None, ("dp", "tensor"), None),
            P(("dp", "tensor")),
            P(None, "dp", None, "tensor"),
            P(None, "tensor", "dp"),
            P(None, "dp", "tensor"),
            P(None, "tensor", "dp"),
        ),
        check_vma=False,
    )
```

profile of v0, /device:TPU:1, one launch (start us, length us, event | category | flops | bytes accessed | tf_op | source)
XLA Modules:
  0.0 1060.1 jit_solution(5597651121133150835)
XLA Ops:
  11.8 10.9 %all-gather = bf16[1,2,768]{1,0,2:T(2,128)(2,1)S(1)} all-gather(bf16[1,2,96]{1,0,2:T(2,128)(2,1)S(1)} %copy.57), channel_id=2, replica_groups=mesh['dp'=8,'tensor'=4] {'dp'}, dimensions={2}, use_global_device_ids=true | all-gather | bytes 3456 | tf_op jit(solution)/shard_map/all_gather | solution.py:81
  22.7 4.6 fusion.132
  30.9 10.4 all-gather.2
  41.8 12.9 %all-gather.1 = bf16[1,768,3,192]{3,2,0,1:T(4,128)(2,1)S(1)} all-gather(bf16[1,96,3,192]{3,2,0,1:T(4,128)(2,1)S(1)} %copy.58), channel_id=3, replica_groups=mesh['dp'=8,'tensor'=4] {'dp'}, dimensions={1}, use_global_device_ids=true | all-gather | bytes 995328 | tf_op jit(solution)/shard_map/all_gather | solution.py:82
  55.5 4.2 fusion.12
  59.7 5.8 all-gather.18.cloned.1.call-done
  65.5 2.5 fusion.161
  68.2 9.5 fusion.159
  77.8 5.8 fusion.64
  83.6 2.4 fusion.142
  86.1 17.0 %all-gather.22.cloned.1.call-done = bf16[1024,768]{1,0:T(8,128)(2,1)} async-done(((bf16[256,768]{1,0:T(8,128)(2,1)}), bf16[1024,768]{1,0:T(8,128)(2,1)}) %all-gather.22.cloned.1.call-update) | async-done | bytes 1572880 | tf_op jit(solution)/shard_map/all_gather | solution.py:90
  103.1 2.5 fusion.162
  106.8 7.5 fusion.160
  114.3 5.9 fusion.70
  121.0 2.3 fusion.140
  124.0 40.5 %reduce-scatter.15.cloned.1.call-done = f32[256,768]{1,0:T(8,128)} async-done(((f32[1024,768]{1,0:T(8,128)}), f32[256,768]{1,0:T(8,128)}) %reduce-scatter.15.cloned.1.call-update) | async-done | bytes 786448 | tf_op jit(solution)/shard_map/reduce_scatter | solution.py:98
  164.5 62.5 %reduce-scatter.19.cloned.1.call-done = f32[256,768]{1,0:T(8,128)} async-done(((f32[1024,768]{1,0:T(8,128)}), f32[256,768]{1,0:T(8,128)}) %reduce-scatter.19.cloned.1.call-update) | async-done | bytes 786448 | tf_op jit(solution)/shard_map/reduce_scatter | solution.py:98
  227.0 2.2 fusion.153
  231.0 2.1 fusion.158
  233.7 33.5 %all-gather.20.cloned.1.call-done = bf16[1024,768]{1,0:T(8,128)(2,1)} async-done(((bf16[256,768]{1,0:T(8,128)(2,1)}), bf16[1024,768]{1,0:T(8,128)(2,1)}) %all-gather.20.cloned.1.call-update) | async-done | bytes 1572880 | tf_op jit(solution)/shard_map/all_gather | solution.py:90
  267.2 11.0 %multiply_convert_fusion.3 = (bf16[1024,768]{1,0:T(8,128)(2,1)}, f32[1024,768]{1,0:T(8,128)}, f32[1024,768]{1,0:T(8,128)}) fusion(bf16[1024,768]{1,0:T(8,128)(2,1)} %all-gather.20.cloned.1.call-done, bf16[1,768,768]{2,1,0:T(8,128)(2,1)} %all-gather.30.cloned.1.call-done), kind=kOutput, calls=%fused_computation.48 | convolution fusion | flops 1259077632 | bytes 10616832 | tf_op jit(solution)/shard_map/dot_general | solution.py:154
  278.1 14.4 %all-gather.32.cloned.1.call-done = bf16[1,768,768]{1,2,0:T(8,128)(2,1)} async-done(((bf16[1,768,96]{1,2,0:T(8,128)(2,1)}), bf16[1,768,768]{1,2,0:T(8,128)(2,1)}) %all-gather.32.cloned.1.call-update) | async-done | bytes 1179664 | tf_op jit(solution)/shard_map/all_gather | solution.py:85
  292.5 38.3 %all-gather.34.cloned.1.call-done = bf16[1,1024,768]{2,1,0:T(8,128)(2,1)} async-done(((bf16[1,256,768]{2,1,0:T(8,128)(2,1)}), bf16[1,1024,768]{2,1,0:T(8,128)(2,1)}) %all-gather.34.cloned.1.call-update) | async-done | bytes 1572880 | tf_op jit(solution)/shard_map/all_gather | solution.py:94
  330.8 5.7 add_convert_fusion.1
  337.6 3.2 fusion.94
  341.7 58.4 %reduce-scatter.23.cloned.1.call-done = f32[256,768]{1,0:T(8,128)} async-done(((f32[1024,768]{1,0:T(8,128)}), f32[256,768]{1,0:T(8,128)}) %reduce-scatter.23.cloned.1.call-update) | async-done | bytes 786448 | tf_op jit(solution)/shard_map/reduce_scatter | solution.py:107
  400.1 2.8 multiply_reduce_fusion.3
  403.8 36.1 %all-gather.24.cloned.1.call-done = bf16[1024,768]{1,0:T(8,128)(2,1)} async-done(((bf16[256,768]{1,0:T(8,128)(2,1)}), bf16[1024,768]{1,0:T(8,128)(2,1)}) %all-gather.24.cloned.1.call-update) | async-done | bytes 1572880 | tf_op jit(solution)/shard_map/all_gather | solution.py:90
  439.9 11.0 %multiply_convert_fusion.2 = (bf16[1024,768]{1,0:T(8,128)(2,1)}, f32[1024,768]{1,0:T(8,128)}, f32[1024,768]{1,0:T(8,128)}) fusion(bf16[1024,768]{1,0:T(8,128)(2,1)} %all-gather.24.cloned.1.call-done, bf16[1,768,768]{2,1,0:T(8,128)(2,1)} %all-gather.30.cloned.1.call-done), kind=kOutput, calls=%fused_computation.31 | convolution fusion | flops 1259077632 | bytes 10616832 | tf_op jit(solution)/shard_map/dot_general | solution.py:154
  450.9 26.3 %all-gather.36.cloned.1.call-done = bf16[1,1024,768]{2,1,0:T(8,128)(2,1)} async-done(((bf16[1,256,768]{2,1,0:T(8,128)(2,1)}), bf16[1,1024,768]{2,1,0:T(8,128)(2,1)}) %all-gather.36.cloned.1.call-update) | async-done | bytes 1572880 | tf_op jit(solution)/shard_map/all_gather | solution.py:94
  477.2 5.7 add_convert_fusion
  484.1 3.0 fusion.92
  487.2 4.9 fusion.90
  492.2 5.4 fusion.88
  498.8 47.9 %reduce-scatter.27.cloned.1.call-done = f32[256,768]{1,0:T(8,128)} async-done(((f32[1024,768]{1,0:T(8,128)}), f32[256,768]{1,0:T(8,128)}) %reduce-scatter.27.cloned.1.call-update) | async-done | bytes 786448 | tf_op jit(solution)/shard_map/reduce_scatter | solution.py:107
  546.7 2.1 multiply_reduce_fusion.2
  549.9 59.2 %reduce-scatter.17.cloned.1.call-done = f32[256,768]{1,0:T(8,128)} async-done(((f32[1024,768]{1,0:T(8,128)}), f32[256,768]{1,0:T(8,128)}) %reduce-scatter.17.cloned.1.call-update) | async-done | bytes 786448 | tf_op jit(solution)/shard_map/reduce_scatter | solution.py:98
  609.1 62.6 %reduce-scatter.21.cloned.1.call-done = f32[256,768]{1,0:T(8,128)} async-done(((f32[1024,768]{1,0:T(8,128)}), f32[256,768]{1,0:T(8,128)}) %reduce-scatter.21.cloned.1.call-update) | async-done | bytes 786448 | tf_op jit(solution)/shard_map/reduce_scatter | solution.py:98
  671.7 4.4 fusion.150
  677.0 36.0 %all-gather.28.cloned.1.call-done = bf16[1024,768]{1,0:T(8,128)(2,1)} async-done(((bf16[256,768]{1,0:T(8,128)(2,1)}), bf16[1024,768]{1,0:T(8,128)(2,1)}) %all-gather.28.cloned.1.call-update) | async-done | bytes 1572880 | tf_op jit(solution)/shard_map/all_gather | solution.py:94
  712.9 2.1 convolution_convert_fusion
  715.1 6.6 fusion.73
  721.7 8.7 multiply_reduce_fusion
  730.4 19.8 %all-gather.26.cloned.1.call-done = bf16[1024,768]{1,0:T(8,128)(2,1)} async-done(((bf16[256,768]{1,0:T(8,128)(2,1)}), bf16[1024,768]{1,0:T(8,128)(2,1)}) %all-gather.26.cloned.1.call-update) | async-done | bytes 1572880 | tf_op jit(solution)/shard_map/all_gather | solution.py:94
  753.9 9.8 multiply_convert_fusion
  763.7 2.0 fusion.63
  767.8 3.2 fusion.164
  771.9 2.1 convolution_convert_fusion.1
  774.0 10.2 multiply_reduce_fusion.1
  786.7 6.7 multiply_convert_fusion.1
  798.9 3.1 fusion.163
  802.1 3.5 fusion.166
  805.6 3.0 convolution_add_fusion
  808.9 3.5 fusion.38
  812.5 3.0 fusion.53
  815.6 3.0 fusion.34
  818.6 2.9 fusion.50
  821.7 2.5 pad_maximum_fusion
  825.8 24.6 %reduce-scatter.29.cloned.1.call-done = f32[256,768]{1,0:T(8,128)} async-done(((f32[1024,768]{1,0:T(8,128)}), f32[256,768]{1,0:T(8,128)}) %reduce-scatter.29.cloned.1.call-update) | async-done | bytes 786448 | tf_op jit(solution)/shard_map/reduce_scatter | solution.py:107
  850.3 62.6 %reduce-scatter.25.cloned.1.call-done = f32[256,768]{1,0:T(8,128)} async-done(((f32[1024,768]{1,0:T(8,128)}), f32[256,768]{1,0:T(8,128)}) %reduce-scatter.25.cloned.1.call-update) | async-done | bytes 786448 | tf_op jit(solution)/shard_map/reduce_scatter | solution.py:107
  912.9 2.1 fusion.130
  915.1 39.8 %all-reduce = f32[1536]{0:T(1024)S(1)} all-reduce(f32[1536]{0:T(1024)S(1)} %add.118), channel_id=17, replica_groups=mesh['dp'=8,'tensor'=4] {'dp','tensor'}, use_global_device_ids=true, to_apply=%region_38.39.clone | all-reduce | flops 1536 | bytes 12288
  959.3 46.7 %reduce-scatter.35.cloned.1.call-done = f32[768,96]{0,1:T(8,128)} async-done(((f32[768,768]{0,1:T(8,128)}), f32[768,96]{0,1:T(8,128)}) %reduce-scatter.35.cloned.1.call-update) | async-done | bytes 294928 | tf_op jit(solution)/shard_map/reduce_scatter | solution.py:122
  1006.0 46.3 %reduce-scatter.31.cloned.1.call-done = f32[96,3,192]{2,0,1:T(8,128)} async-done(((f32[768,3,192]{2,0,1:T(8,128)}), f32[96,3,192]{2,0,1:T(8,128)}) %reduce-scatter.31.cloned.1.call-update) | async-done | bytes 221200 | tf_op jit(solution)/shard_map/reduce_scatter | solution.py:119
  (219 shorter events, 42.0 us)
Async XLA Ops:
  8.0 19.4 %copy-start = (bf16[2,256,768]{2,1,0:T(8,128)(2,1)S(1)}, bf16[2,256,768]{2,1,0:T(8,128)(2,1)}, u32[]{:S(2)}) copy-start(bf16[2,256,768]{2,1,0:T(8,128)(2,1)} %param.9) | copy-start | bytes 2359300
  8.0 21.4 %copy-start.46 = (s32[2,1,4]{2,1,0:T(1,128)S(1)}, s32[2,1,4]{2,1,0:T(1,128)}, u32[]{:S(2)}) copy-start(s32[2,1,4]{2,1,0:T(1,128)} %param.11) | copy-start | bytes 100
  8.0 21.7 %copy-start.44 = (s32[2,1024]{1,0:T(2,128)S(1)}, s32[2,1024]{1,0:T(2,128)}, u32[]{:S(2)}) copy-start(s32[2,1024]{1,0:T(2,128)} %param.12) | copy-start | bytes 24580
  8.0 22.6 %copy-start.29 = (bf16[1,192,96]{2,1,0:T(8,128)(2,1)S(1)}, bf16[1,192,96]{2,1,0:T(8,128)(2,1)}, u32[]{:S(2)}) copy-start(bf16[1,192,96]{2,1,0:T(8,128)(2,1)} %param.15) | copy-start | bytes 110596
  8.0 22.7 %copy-start.26 = (bf16[1,96,3,192]{3,1,2,0:T(8,128)(2,1)S(1)}, bf16[1,96,3,192]{3,1,2,0:T(8,128)(2,1)}, u32[]{:S(2)}) copy-start(bf16[1,96,3,192]{3,1,2,0:T(8,128)(2,1)} %param.14) | copy-start | bytes 331780
  8.1 57.5 %all-gather.18.cloned.1.call-start = ((), (), s32[]{:S(2)}) async-start(), calls=%async_computation.12 | async-start | bytes 1966080 | tf_op jit(solution)/shard_map/all_gather | solution.py:90
  9.5 21.0 %copy-start.30 = (f32[256]{0:T(256)}, f32[256]{0:T(256)S(1)}, u32[]{:S(2)}) copy-start(f32[256]{0:T(256)S(1)} %get-tuple-element.66) | copy-start | bytes 3076
  9.5 21.0 %copy-start.32 = (f32[256]{0:T(256)}, f32[256]{0:T(256)S(1)}, u32[]{:S(2)}) copy-start(f32[256]{0:T(256)S(1)} %get-tuple-element.67) | copy-start | bytes 3076
  11.0 19.5 %copy-start.37 = (f32[256]{0:T(256)}, f32[256]{0:T(256)S(1)}, u32[]{:S(2)}) copy-start(f32[256]{0:T(256)S(1)} %add_rsqrt_fusion.3) | copy-start | bytes 3076
  11.0 19.5 %copy-start.39 = (f32[256]{0:T(256)}, f32[256]{0:T(256)S(1)}, u32[]{:S(2)}) copy-start(f32[256]{0:T(256)S(1)} %add_rsqrt_fusion.1) | copy-start | bytes 3076
  27.4 3.1 copy-start.27
  28.6 74.5 %all-gather.22.cloned.1.call-start = ((), (), s32[]{:S(2)}) async-start(), calls=%async_computation.16 | async-start | bytes 1966080 | tf_op jit(solution)/shard_map/all_gather | solution.py:90
  29.3 135.2 %reduce-scatter.15.cloned.1.call-start = ((), (), s32[]{:S(2)}) async-start(), calls=%async_computation.13 | async-start | bytes 3932160 | tf_op jit(solution)/shard_map/reduce_scatter | solution.py:98
  41.7 41.9 %copy-start.6 = (bf16[1,192,768]{2,1,0:T(8,128)(2,1)}, bf16[1,192,768]{2,1,0:T(8,128)(2,1)S(1)}, u32[]{:S(2)}) copy-start(bf16[1,192,768]{2,1,0:T(8,128)(2,1)S(1)} %copy.62) | copy-start | bytes 884740
  55.5 47.6 %copy-start.19 = (bf16[1,768,3,192]{1,3,2,0:T(8,128)(2,1)}, bf16[1,768,3,192]{1,3,2,0:T(8,128)(2,1)S(1)}, u32[]{:S(2)}) copy-start(bf16[1,768,3,192]{1,3,2,0:T(8,128)(2,1)S(1)} %copy.59) | copy-start | bytes 2654212
  68.2 9.5 copy-start.2
  86.0 141.0 %reduce-scatter.19.cloned.1.call-start = ((), (), s32[]{:S(2)}) async-start(), calls=%async_computation.17 | async-start | bytes 3932160 | tf_op jit(solution)/shard_map/reduce_scatter | solution.py:98
  114.3 5.9 copy-start.35
  114.3 6.7 copy-start.7
  123.4 110.2 %all-gather.30.cloned.1.call-start = ((), (), s32[]{:S(2)}) async-start(), calls=%async_computation.29 | async-start | bytes 1327104 | tf_op jit(solution)/shard_map/all_gather | solution.py:84
  124.0 143.2 %all-gather.20.cloned.1.call-start = ((), (), s32[]{:S(2)}) async-start(), calls=%async_computation.14 | async-start | bytes 1966080 | tf_op jit(solution)/shard_map/all_gather | solution.py:90
  230.3 62.2 %all-gather.32.cloned.1.call-start = ((), (), s32[]{:S(2)}) async-start(), calls=%async_computation.30 | async-start | bytes 1327104 | tf_op jit(solution)/shard_map/all_gather | solution.py:85
  230.9 99.9 %all-gather.34.cloned.1.call-start = ((), (), s32[]{:S(2)}) async-start(), calls=%async_computation.31 | async-start | bytes 1966080 | tf_op jit(solution)/shard_map/all_gather | solution.py:94
  233.0 167.1 %reduce-scatter.23.cloned.1.call-start = ((), (), s32[]{:S(2)}) async-start(), calls=%async_computation.20 | async-start | bytes 3932160 | tf_op jit(solution)/shard_map/reduce_scatter | solution.py:107
  330.8 6.8 copy-start.50
  340.8 99.1 %all-gather.24.cloned.1.call-start = ((), (), s32[]{:S(2)}) async-start(), calls=%async_computation.18 | async-start | bytes 1966080 | tf_op jit(solution)/shard_map/all_gather | solution.py:90
  341.7 204.9 %copy-start.41 = (f32[256]{0:T(256)}, f32[256]{0:T(256)S(1)}, u32[]{:S(2)}) copy-start(f32[256]{0:T(256)S(1)} %add_rsqrt_fusion) | copy-start | bytes 3076
  403.0 74.2 %all-gather.36.cloned.1.call-start = ((), (), s32[]{:S(2)}) async-start(), calls=%async_computation.32 | async-start | bytes 1966080 | tf_op jit(solution)/shard_map/all_gather | solution.py:94
  403.6 143.0 %reduce-scatter.27.cloned.1.call-start = ((), (), s32[]{:S(2)}) async-start(), calls=%async_computation.23 | async-start | bytes 3932160 | tf_op jit(solution)/shard_map/reduce_scatter | solution.py:107
  477.2 6.9 copy-start.51
  487.1 122.0 %reduce-scatter.17.cloned.1.call-start = ((), (), s32[]{:S(2)}) async-start(), calls=%async_computation.15 | async-start | bytes 3932160 | tf_op jit(solution)/shard_map/reduce_scatter | solution.py:98
  492.1 179.6 %reduce-scatter.21.cloned.1.call-start = ((), (), s32[]{:S(2)}) async-start(), calls=%async_computation.19 | async-start | bytes 3932160 | tf_op jit(solution)/shard_map/reduce_scatter | solution.py:98
  497.6 215.4 %all-gather.28.cloned.1.call-start = ((), (), s32[]{:S(2)}) async-start(), calls=%async_computation.24 | async-start | bytes 1966080 | tf_op jit(solution)/shard_map/all_gather | solution.py:94
  676.1 74.1 %all-gather.26.cloned.1.call-start = ((), (), s32[]{:S(2)}) async-start(), calls=%async_computation.21 | async-start | bytes 1966080 | tf_op jit(solution)/shard_map/all_gather | solution.py:94
  676.7 147.4 %reduce-scatter.37.cloned.1.call-start = ((), (), s32[]{:S(2)}) async-start(), calls=%async_computation.33 | async-start | bytes 884736
  715.0 6.6 copy-start.36
  721.7 45.3 %copy-start.22 = (bf16[3,64,1024]{2,1,0:T(8,128)(2,1)}, bf16[3,64,1024]{2,1,0:T(8,128)(2,1)S(1)}, u32[]{:S(2)}) copy-start(bf16[3,64,1024]{2,1,0:T(8,128)(2,1)S(1)} %fusion.73) | copy-start | bytes 1179652
  721.7 28.5 %copy-start.10 = (bf16[3,64,1024]{2,1,0:T(8,128)(2,1)S(1)}, bf16[3,64,1024]{2,1,0:T(8,128)(2,1)}, u32[]{:S(2)}) copy-start(bf16[3,64,1024]{2,1,0:T(8,128)(2,1)} %copy-done.9) | copy-start | bytes 1179652
  721.7 30.5 %copy-start.12 = (bf16[3,64,1024]{2,1,0:T(8,128)(2,1)S(1)}, bf16[3,64,1024]{2,1,0:T(8,128)(2,1)}, u32[]{:S(2)}) copy-start(bf16[3,64,1024]{2,1,0:T(8,128)(2,1)} %copy-done.11) | copy-start | bytes 1179652
  753.9 96.4 %reduce-scatter.29.cloned.1.call-start = ((), (), s32[]{:S(2)}) async-start(), calls=%async_computation.25 | async-start | bytes 3932160 | tf_op jit(solution)/shard_map/reduce_scatter | solution.py:107
  770.9 3.0 copy-start.3
  770.9 3.1 copy-start.34
  771.0 141.9 %reduce-scatter.25.cloned.1.call-start = ((), (), s32[]{:S(2)}) async-start(), calls=%async_computation.22 | async-start | bytes 3932160 | tf_op jit(solution)/shard_map/reduce_scatter | solution.py:107
  774.0 10.3 slice-start
  774.0 11.5 %slice-start.1 = ((s8[12582912]{0:T(1024)(128)(4,1)}), s8[4194304]{0:T(1024)(128)(4,1)S(1)}, s32[]{:S(2)}) async-start(s8[12582912]{0:T(1024)(128)(4,1)} %bitcast.298), calls=%async_computation.35 | async-start | bytes 8388608
  774.0 12.7 %slice-start.2 = ((s8[12582912]{0:T(1024)(128)(4,1)}), s8[4194304]{0:T(1024)(128)(4,1)S(1)}, s32[]{:S(2)}) async-start(s8[12582912]{0:T(1024)(128)(4,1)} %bitcast.298), calls=%async_computation.36 | async-start | bytes 8388608
  798.7 3.3 copy-start.24
  802.0 157.3 %reduce-scatter.33.cloned.1.call-start = ((), (), s32[]{:S(2)}) async-start(), calls=%async_computation.27 | async-start | bytes 2654208 | tf_op jit(solution)/shard_map/reduce_scatter | solution.py:121
  802.1 3.6 copy-start.49
  802.1 3.6 copy-start.53
  808.7 197.3 %reduce-scatter.35.cloned.1.call-start = ((), (), s32[]{:S(2)}) async-start(), calls=%async_computation.28 | async-start | bytes 2654208 | tf_op jit(solution)/shard_map/reduce_scatter | solution.py:122
  808.9 3.6 copy-start.48
  808.9 3.6 copy-start.54
  812.5 3.1 copy-start.14
  812.5 3.1 copy-start.16
  812.5 3.1 copy-start.23
  815.5 236.8 %reduce-scatter.31.cloned.1.call-start = ((), (), s32[]{:S(2)}) async-start(), calls=%async_computation.26 | async-start | bytes 2654208 | tf_op jit(solution)/shard_map/reduce_scatter | solution.py:119
  821.5 91.3 %copy-start.1 = (bf16[2,256,768]{2,1,0:T(8,128)(2,1)S(1)}, bf16[2,256,768]{2,1,0:T(8,128)(2,1)}, u32[]{:S(2)}) copy-start(bf16[2,256,768]{2,1,0:T(8,128)(2,1)} %param.9) | copy-start | bytes 2359300
  821.5 91.3 %copy-start.28 = (f32[768]{0:T(1024)S(1)}, f32[768]{0:T(1024)}, u32[]{:S(2)}) copy-start(f32[768]{0:T(1024)} %copy-done.27) | copy-start | bytes 9220
  821.5 91.3 %copy-start.31 = (f32[256]{0:T(256)S(1)}, f32[256]{0:T(256)}, u32[]{:S(2)}) copy-start(f32[256]{0:T(256)} %copy-done.30) | copy-start | bytes 3076
  821.5 91.3 %copy-start.33 = (f32[256]{0:T(256)S(1)}, f32[256]{0:T(256)}, u32[]{:S(2)}) copy-start(f32[256]{0:T(256)} %copy-done.32) | copy-start | bytes 3076
  821.5 91.4 %copy-start.38 = (f32[256]{0:T(256)S(1)}, f32[256]{0:T(256)}, u32[]{:S(2)}) copy-start(f32[256]{0:T(256)} %copy-done.37) | copy-start | bytes 3076
  821.5 91.4 %copy-start.40 = (f32[256]{0:T(256)S(1)}, f32[256]{0:T(256)}, u32[]{:S(2)}) copy-start(f32[256]{0:T(256)} %copy-done.39) | copy-start | bytes 3076
  821.6 133.9 %copy-start.4 = (f32[256,768]{1,0:T(8,128)S(1)}, f32[256,768]{1,0:T(8,128)}, u32[]{:S(2)}) copy-start(f32[256,768]{1,0:T(8,128)} %get-tuple-element.44) | copy-start | bytes 2359300
  (17 other events, 31.7 us)
Sparse Core Ops, SparseCore 0:
  28.7 36.7 all-gather.17
  67.1 35.9 all-gather.21
  105.4 59.0 reduce-scatter.14
  166.7 60.2 reduce-scatter.18
  487.3 59.3 reduce-scatter.26
  548.8 60.2 reduce-scatter.16
  611.4 60.2 reduce-scatter.20
Sparse Core Ops, SparseCore 1:
  125.8 23.2 all-gather.29
  230.4 36.7 all-gather.19
  268.9 23.6 all-gather.31
  294.7 36.1 all-gather.33
  340.9 59.2 reduce-scatter.22
  403.1 36.8 all-gather.23
  441.4 35.8 all-gather.35
  676.2 36.7 all-gather.27
  714.4 35.8 all-gather.25
  754.0 33.7 reduce-scatter.36
  789.9 60.3 reduce-scatter.28
  852.6 60.2 reduce-scatter.24
  916.7 42.5 reduce-scatter.32
  963.6 42.4 reduce-scatter.34
  1009.9 42.3 reduce-scatter.30
where the time goes:
time: 1070 us; the launch traced here: 1060 us
  waiting for transfers between devices  742 us (69%)
  matrix products  154 us (14%)
  blocking collectives  74 us (7%)
  other arithmetic  54 us (5%)
  between operations  17.1 us (2%)
  local copies, waits for them, and re-layouts  16.2 us (2%)
    reduce_scatter x4, waiting for transfers between devices, collect_rows(): lax.psum_scatter(jnp.dot(operand, weight, preferred_element_type=jnp.floa...  225 us
    reduce_scatter x4, waiting for transfers between devices, return_rows(): lax.psum_scatter(lax.dot_general(operand, weight, (((1,), (1,)), ((), ())...  193 us
    all_gather x4, waiting for transfers between devices, spread_grad(): return lax.all_gather(block_rows, 'tensor', axis=0, tiled=True)  120 us
    all_gather x4, waiting for transfers between devices, spread(): return lax.all_gather(block_rows, 'tensor', axis=0, tiled=True)  92.4 us
    reduce_scatter x1, waiting for transfers between devices, reduce_grads(): lax.psum_scatter(pieces[3], 'dp', scatter_dimension=1, tiled=True)  46.7 us
    reduce_scatter x1, waiting for transfers between devices, reduce_grads(): lax.psum_scatter(pieces[0], 'dp', scatter_dimension=0, tiled=True)  46.3 us
    unnamed x1, blocking collectives  39.8 us
    dot_general x2, matrix products, body(): jnp.dot(second_input, up_weight, preferred_element_type=jnp.float32)  22 us
  transfers between devices with their start and end apart: 22, of which 20 were waited for; matrix products, arithmetic and copies ran while one was open for 17% of the time, Pallas kernels for 0%

commit v1 on v0

--- a/solution.py
+++ b/solution.py
@@ -1,14 +1,369 @@
+import functools
+
 import jax
 import jax.numpy as jnp
 from jax import lax
+from jax.experimental import pallas as pl
+from jax.experimental.pallas import tpu as pltpu
 from jax.sharding import PartitionSpec as P
 
 D = 768
 HD = 64
-
-
 NEGATIVE = -1e30
 EPSILON = 1e-06
+MESH = pl.DeviceIdType.MESH
+F32 = jnp.float32
+BF16 = jnp.bfloat16
+KINDS = 3
+
+
+def flip(value, bit):
+    size = 1 << bit
+    return value + size * (1 - 2 * ((value // size) % 2))
+
+
+def flip_mask(value, mask):
+    bit = 0
+    while mask >> bit:
+        if (mask >> bit) & 1:
+            value = flip(value, bit)
+        bit += 1
+    return value
+
+
+def submasks(bits):
+    masks = [0]
+    for bit in bits:
+        masks = masks + [mask | (1 << bit) for mask in masks]
+    return masks
+
+
+def color_order(color, bit_count):
+    order = list(range(bit_count))
+    return order if color == 0 else order[::-1]
+
+
+class Place:
+    def __init__(self, depth):
+        dp = lax.axis_index("dp")
+        self.z = lax.axis_index("tensor")
+        self.c = dp % 2
+        self.p = dp // 2
+        self.depth = depth
+
+    def same(self, p, c, z):
+        return jnp.logical_and(c == self.c, z == self.z)
+
+
+def device(p, c, z):
+    return (2 * p + c, z)
+
+
+def rows_of(p, color, shard):
+    return pl.ds(pl.multiple_of((2 * p + color) * shard, 16), shard)
+
+
+def send_or_copy(is_self, source, target, send_sem, recv_sem, dest):
+    @pl.when(is_self)
+    def _():
+        pltpu.make_async_copy(source, target, recv_sem).start()
+
+    @pl.when(jnp.logical_not(is_self))
+    def _():
+        pltpu.make_async_remote_copy(
+            source, target, send_sem, recv_sem, device_id=dest, device_id_type=MESH
+        ).start()
+
+
+def wait_send_if(is_self, source, send_sem):
+    @pl.when(jnp.logical_not(is_self))
+    def _():
+        pltpu.make_async_copy(source, source, send_sem).wait()
+
+
+def wait_bytes(ref, sem):
+    pltpu.make_async_copy(ref, ref, sem).wait()
+
+
+def entry_barrier(here, depth, bit_count):
+    barrier = pltpu.get_barrier_semaphore()
+    count = 0
+    for dz in range(depth):
+        for dc in range(2):
+            if dz == 0 and dc == 0:
+                continue
+            other_core = here.c if dc == 0 else 1 - here.c
+            pl.semaphore_signal(
+                barrier,
+                inc=1,
+                device_id=device(here.p, other_core, (here.z + dz) % depth),
+                device_id_type=MESH,
+            )
+            count += 1
+    for bit in range(bit_count):
+        pl.semaphore_signal(
+            barrier,
+            inc=1,
+            device_id=device(flip(here.p, bit), here.c, here.z),
+            device_id_type=MESH,
+        )
+        count += 1
+    pl.semaphore_wait(barrier, count)
+
+
+def gather_kernel(depth, bit_count, shard, tok, cot, packed, x_out, dy_out, w_out, *sems):
+    tok_s, tok_r, z_s, z_r, x_s, x_r = sems
+    here = Place(depth)
+    half = depth // 2
+    entry_barrier(here, depth, bit_count)
+    waits = []
+
+    def send_rows(which, array, target):
+        for m in range(2):
+            to_z = 2 * m + here.c
+            to_c = here.z // half
+            is_self = here.same(here.p, to_c, to_z)
+            slot = here.z % half
+            send_or_copy(
+                is_self,
+                array.at[m],
+                target.at[slot],
+                tok_s.at[which, m],
+                tok_r.at[which, slot],
+                device(here.p, to_c, to_z),
+            )
+            waits.append(functools.partial(wait_send_if, is_self, array.at[m], tok_s.at[which, m]))
+
+    def send_z(k):
+        for dz in range(depth):
+            to_z = (here.z + dz) % depth
+            to_c = here.z // half
+            is_self = here.same(here.p, to_c, to_z)
+            slot = here.z % half
+            send_or_copy(
+                is_self,
+                packed.at[k],
+                w_out.at[k, slot, rows_of(here.p, here.c, shard)],
+                z_s.at[k, dz],
+                z_r.at[k, here.c, slot],
+                device(here.p, to_c, to_z),
+            )
+            waits.append(functools.partial(wait_send_if, is_self, packed.at[k], z_s.at[k, dz]))
+
+    def wait_z(k, color):
+        for slot in range(half):
+            wait_bytes(w_out.at[k, slot, rows_of(here.p, color, shard)], z_r.at[k, color, slot])
+
+    def step(k, color, s):
+        order = color_order(color, bit_count)
+        for index, mask in enumerate(submasks(order[:s])):
+            block = w_out.at[k, :, rows_of(flip_mask(here.p, mask), color, shard)]
+            pltpu.make_async_remote_copy(
+                block,
+                block,
+                x_s.at[k, color, s, index],
+                x_r.at[k, color, s, index],
+                device_id=device(flip(here.p, order[s]), here.c, here.z),
+                device_id_type=MESH,
+            ).start()
+            waits.append(functools.partial(wait_bytes, block, x_s.at[k, color, s, index]))
+
+    def wait_step(k, color, s):
+        order = color_order(color, bit_count)
+        for index, mask in enumerate(submasks(order[:s])):
+            landed = flip(flip_mask(here.p, mask), order[s])
+            wait_bytes(
+                w_out.at[k, :, rows_of(landed, color, shard)], x_r.at[k, color, s, index]
+            )
+
+    send_z(0)
+    send_rows(0, tok, x_out)
+    send_z(1)
+    send_z(2)
+    send_rows(1, cot, dy_out)
+    total = KINDS + bit_count
+    for time in range(total + 1):
+        for k in range(KINDS):
+            s = time - k
+            for color in range(2):
+                if s == 0:
+                    wait_z(k, color)
+                elif 0 < s <= bit_count:
+                    wait_step(k, color, s - 1)
+                if 0 <= s < bit_count:
+                    step(k, color, s)
+    for which, target in ((0, x_out), (1, dy_out)):
+        for slot in range(half):
+            wait_bytes(target.at[slot], tok_r.at[which, slot])
+    for wait in waits:
+        wait()
+
+
+def gather_all(mesh, tok, cot, packed):
+    depth = mesh.shape["tensor"]
+    bit_count = (mesh.shape["dp"] // 2).bit_length() - 1
+    shard = packed.shape[1]
+    half = depth // 2
+    vmem = pl.BlockSpec(memory_space=pltpu.VMEM)
+    sem = pltpu.SemaphoreType.DMA
+    blocks = 1 << (bit_count - 1)
+    return pl.pallas_call(
+        functools.partial(gather_kernel, depth, bit_count, shard),
+        out_shape=(
+            jax.ShapeDtypeStruct((half,) + tok.shape[1:], BF16),
+            jax.ShapeDtypeStruct((half,) + tok.shape[1:], BF16),
+            jax.ShapeDtypeStruct((KINDS, half, D, packed.shape[2]), BF16),
+        ),
+        in_specs=[vmem] * 3,
+        out_specs=(vmem,) * 3,
+        scratch_shapes=[
+            sem((2, 2)),
+            sem((2, half)),
+            sem((KINDS, depth)),
+            sem((KINDS, 2, half)),
+            sem((KINDS, 2, bit_count, blocks)),
+            sem((KINDS, 2, bit_count, blocks)),
+        ],
+        compiler_params=pltpu.CompilerParams(
+            collective_id=0, has_side_effects=True, vmem_limit_bytes=40 << 20
+        ),
+        name="gather_all",
+    )(tok, cot, packed)
+
+
+def scatter_kernel(
+    depth, bit_count, shard, grads, y, dx, g_out, y_out, dx_out, held, rx, zrx, copy_sem, *sems
+):
+    row_s, row_r, z_s, z_r, x_s, x_r = sems
+    here = Place(depth)
+    half = depth // 2
+    pltpu.make_async_copy(grads, held, copy_sem).start()
+    entry_barrier(here, depth, bit_count)
+    waits = []
+
+    def send_rows(which, array, target):
+        for slot in range(half):
+            to_c = here.z % 2
+            to_z = half * here.c + slot
+            is_self = here.same(here.p, to_c, to_z)
+            m = here.z // 2
+            send_or_copy(
+                is_self,
+                array.at[slot],
+                target.at[m],
+                row_s.at[which, slot],
+                row_r.at[which, m],
+                device(here.p, to_c, to_z),
+            )
+            waits.append(
+                functools.partial(wait_send_if, is_self, array.at[slot], row_s.at[which, slot])
+            )
+
+    def order_of(color):
+        return color_order(color, bit_count)[::-1]
+
+    def step(k, color, s):
+        order = order_of(color)
+        bit = order[s]
+        for index, mask in enumerate(submasks(order[s + 1 :])):
+            block = held.at[k, :, rows_of(flip_mask(flip(here.p, bit), mask), color, shard)]
+            pltpu.make_async_remote_copy(
+                block,
+                rx.at[k, color, (1 << bit_count) - (1 << (bit_count - s)) + index],
+                x_s.at[k, color, s, index],
+                x_r.at[k, color, s, index],
+                device_id=device(flip(here.p, bit), here.c, here.z),
+                device_id_type=MESH,
+            ).start()
+            waits.append(functools.partial(wait_bytes, block, x_s.at[k, color, s, index]))
+
+    def finish_step(k, color, s):
+        order = order_of(color)
+        for index, mask in enumerate(submasks(order[s + 1 :])):
+            got = rx.at[k, color, (1 << bit_count) - (1 << (bit_count - s)) + index]
+            wait_bytes(got, x_r.at[k, color, s, index])
+            block = held.at[k, :, rows_of(flip_mask(here.p, mask), color, shard)]
+            block[...] = (block[...].astype(F32) + got[...].astype(F32)).astype(BF16)
+
+    def send_z(k, color):
+        for slot in range(half):
+            to_z = half * here.c + slot
+            is_self = here.same(here.p, color, to_z)
+            block = held.at[k, slot, rows_of(here.p, color, shard)]
+            send_or_copy(
+                is_self,
+                block,
+                zrx.at[k, here.z],
+                z_s.at[k, color, slot],
+                z_r.at[k, here.z],
+                device(here.p, color, to_z),
+            )
+            waits.append(functools.partial(wait_send_if, is_self, block, z_s.at[k, color, slot]))
+
+    def finish_z(k):
+        for source in range(depth):
+            wait_bytes(zrx.at[k, source], z_r.at[k, source])
+        total = zrx[k, 0].astype(F32)
+        for source in range(1, depth):
+            total = total + zrx[k, source].astype(F32)
+        g_out[k] = total
+
+    send_rows(0, y, y_out)
+    send_rows(1, dx, dx_out)
+    pltpu.make_async_copy(grads, held, copy_sem).wait()
+    for time in range(KINDS + bit_count + 1):
+        for k in reversed(range(KINDS)):
+            s = time - (KINDS - 1 - k)
+            for color in range(2):
+                if 0 < s <= bit_count:
+                    finish_step(k, color, s - 1)
+                if 0 <= s < bit_count:
+                    step(k, color, s)
+                elif s == bit_count:
+                    send_z(k, color)
+    for k in reversed(range(KINDS)):
+        finish_z(k)
+    for which, target in ((0, y_out), (1, dx_out)):
+        for m in range(2):
+            wait_bytes(target.at[m], row_r.at[which, m])
+    for wait in waits:
+        wait()
+
+
+def scatter_all(mesh, grads, y, dx, shard):
+    depth = mesh.shape["tensor"]
+    bit_count = (mesh.shape["dp"] // 2).bit_length() - 1
+    half = depth // 2
+    vmem = pl.BlockSpec(memory_space=pltpu.VMEM)
+    sem = pltpu.SemaphoreType.DMA
+    blocks = 1 << (bit_count - 1)
+    width = grads.shape[3]
+    return pl.pallas_call(
+        functools.partial(scatter_kernel, depth, bit_count, shard),
+        out_shape=(
+            jax.ShapeDtypeStruct((KINDS, shard, width), F32),
+            jax.ShapeDtypeStruct(y.shape, BF16),
+            jax.ShapeDtypeStruct(dx.shape, BF16),
+        ),
+        in_specs=[pl.BlockSpec(memory_space=pl.ANY), vmem, vmem],
+        out_specs=(vmem,) * 3,
+        scratch_shapes=[
+            pltpu.VMEM(grads.shape, BF16),
+            pltpu.VMEM((KINDS, 2, (1 << bit_count) - 1, half, shard, width), BF16),
+            pltpu.VMEM((KINDS, depth, shard, width), BF16),
+            sem(()),
+            sem((2, half)),
+            sem((2, 2)),
+            sem((KINDS, 2, half)),
+            sem((KINDS, depth)),
+            sem((KINDS, 2, bit_count, blocks)),
+            sem((KINDS, 2, bit_count, blocks)),
+        ],
+        compiler_params=pltpu.CompilerParams(
+            collective_id=1, has_side_effects=True, vmem_limit_bytes=60 << 20
+        ),
+        name="scatter_all",
+    )(grads, y, dx)
 
 
 def normalize(row_block):
@@ -74,6 +429,143 @@
         * scaling
     )
     return jnp.stack([grad_queries, grad_keys, grad_values], axis=1).astype(jnp.bfloat16)
+
+
+def block_body(mesh, tokens, cotangent, lengths, padding, ln_gain, w_qkv, w_out, w_up, w_down):
+    dp_size, depth = mesh.shape["dp"], mesh.shape["tensor"]
+    half = depth // 2
+    core = lax.axis_index("dp") % 2
+    z = lax.axis_index("tensor")
+    swap = [(i, i ^ 1) for i in range(dp_size)]
+
+    def partner(value):
+        return lax.ppermute(value, "dp", swap)
+
+    def pair_gather(own):
+        other = partner(own)
+        return jnp.concatenate(
+            [jnp.where(core == 0, own, other), jnp.where(core == 0, other, own)], axis=0
+        )
+
+    def pair_scatter(partial):
+        rows = partial.shape[0] // 2
+        parts = partial.reshape(2, rows, -1)
+        own = lax.dynamic_index_in_dim(parts, core, 0, keepdims=False)
+        other = lax.dynamic_index_in_dim(parts, 1 - core, 0, keepdims=False)
+        return own + partner(other.astype(BF16)).astype(F32)
+
+    shard = w_up.shape[1]
+    hid = w_up.shape[2]
+    heads_width = w_qkv.shape[3]
+    packed = jnp.stack(
+        [
+            jnp.concatenate([w_qkv[0].reshape(shard, 3 * heads_width), w_out[0].T], axis=1),
+            w_up[0],
+            w_down[0].T,
+        ]
+    )
+    gains = lax.all_gather(ln_gain[0], "dp", axis=1, tiled=True).astype(F32)
+    gain_first, gain_second = gains[0], gains[1]
+    other_lengths = partner(lengths)
+    other_padding = partner(padding)
+    micro = z // 2
+    mine = (z % 2) == core
+    use_lengths = jnp.where(mine, lengths, other_lengths)[:, 0]
+    use_padding = jnp.where(mine, padding, other_padding)
+    allowed = visible(
+        lax.dynamic_index_in_dim(use_lengths, micro, 0, keepdims=False),
+        lax.dynamic_index_in_dim(use_padding, micro, 0, keepdims=False),
+    )
+
+    x_rows, dy_rows, gathered = gather_all(mesh, tokens, cotangent, packed)
+    entering = x_rows.reshape(-1, D).astype(F32)
+    first = gathered[0]
+    qkv_weight = first[:, :, : 3 * heads_width]
+    out_weight_t = first[:, :, 3 * heads_width :]
+    up_weight = gathered[1]
+    down_weight_t = gathered[2]
+
+    normed, inverse = normalize(entering)
+    first_input = pair_gather((normed * gain_first).astype(BF16))
+    triple = jnp.einsum("rd,hdn->hrn", first_input, qkv_weight, preferred_element_type=F32).astype(
+        BF16
+    )
+    rows = first_input.shape[0]
+    stacked = (
+        triple.reshape(half, rows, 3, -1, HD).transpose(1, 2, 0, 3, 4).reshape(rows, 3, -1, HD)
+    )
+    mixture, highest, totals = attend(stacked, allowed)
+    mix_rounded = mixture.reshape(rows, half, -1).astype(BF16)
+    middle = entering + pair_scatter(
+        jnp.einsum("rhn,hdn->rd", mix_rounded, out_weight_t, preferred_element_type=F32)
+    )
+    normed_two, inverse_two = normalize(middle)
+    second_input = pair_gather((normed_two * gain_second).astype(BF16))
+    hidden_pre = jnp.einsum("rd,hdn->hrn", second_input, up_weight, preferred_element_type=F32)
+    activated = gelu_exact(hidden_pre).astype(BF16)
+    layer_rows = middle + pair_scatter(
+        jnp.einsum("hrn,hdn->rd", activated, down_weight_t, preferred_element_type=F32)
+    )
+
+    incoming = dy_rows.reshape(-1, D).astype(F32)
+    grad_down = pair_gather(dy_rows.reshape(-1, D))
+    down_part = jnp.einsum("rd,hrn->hdn", grad_down, activated, preferred_element_type=F32)
+    grad_act = jnp.einsum("rd,hdn->hrn", grad_down, down_weight_t, preferred_element_type=F32)
+    pulled = jax.vjp(gelu_exact, hidden_pre)
+    grad_pre = pulled[1](grad_act)[0].astype(BF16)
+    up_part = jnp.einsum("rd,hrn->hdn", second_input, grad_pre, preferred_element_type=F32)
+    grad_norm_two = pair_scatter(
+        jnp.einsum("hrn,hdn->rd", grad_pre, up_weight, preferred_element_type=F32)
+    )
+    gain_two_part = jnp.sum(grad_norm_two * normed_two, axis=0)
+    incoming = incoming + norm_back(grad_norm_two, gain_second, normed_two, inverse_two)
+    grad_branch = pair_gather(incoming.astype(BF16))
+    out_part = jnp.einsum("rd,rhn->hdn", grad_branch, mix_rounded, preferred_element_type=F32)
+    grad_mix = (
+        jnp.einsum("rd,hdn->rhn", grad_branch, out_weight_t, preferred_element_type=F32)
+        .astype(BF16)
+        .reshape(rows, -1, HD)
+    )
+    grad_triple = attend_back(stacked, allowed, highest, totals, grad_mix)
+    flat_triple = (
+        grad_triple.reshape(rows, 3, half, -1).transpose(2, 0, 1, 3).reshape(half, rows, -1)
+    )
+    qkv_part = jnp.einsum("rd,hrn->hdn", first_input, flat_triple, preferred_element_type=F32)
+    grad_norm_one = pair_scatter(
+        jnp.einsum("hrn,hdn->rd", flat_triple, qkv_weight, preferred_element_type=F32)
+    )
+    gain_one_part = jnp.sum(grad_norm_one * normed, axis=0)
+    incoming = incoming + norm_back(grad_norm_one, gain_first, normed, inverse)
+    grads = jnp.stack(
+        [
+            jnp.concatenate([qkv_part.astype(BF16), out_part.astype(BF16)], axis=2),
+            up_part.astype(BF16),
+            down_part.astype(BF16),
+        ]
+    )
+    shape = x_rows.shape
+    summed, y_back, dx_back = scatter_all(
+        mesh,
+        grads,
+        layer_rows.astype(BF16).reshape(shape),
+        incoming.astype(BF16).reshape(shape),
+        shard,
+    )
+    gain_flat = jnp.concatenate([gain_one_part, gain_two_part])
+    gain_result = lax.psum_scatter(gain_flat, ("dp", "tensor"), scatter_dimension=0, tiled=True)
+    qkv_grad = summed[0, :, : 3 * heads_width].reshape(1, shard, 3, heads_width)
+    out_grad = summed[0, :, 3 * heads_width :].T[None]
+    up_grad = summed[1][None]
+    down_grad = summed[2].T[None]
+    return (
+        y_back.astype(F32),
+        dx_back.astype(F32),
+        gain_result,
+        qkv_grad,
+        out_grad,
+        up_grad,
+        down_grad,
+    )
 
 
 def collect_weights(ln_gain, w_qkv, w_out, w_up, w_down, layer_index):
@@ -252,9 +744,18 @@
     return (layer_out, input_grad, gain_result, qkv_grad, out_grad, up_grad, down_grad)
 
 
+def fits(mesh):
+    dp_size, depth = mesh.shape["dp"], mesh.shape["tensor"]
+    columns = dp_size // 2
+    return (
+        depth == 4 and dp_size >= 4 and columns & (columns - 1) == 0 and D % (dp_size * 16) == 0
+    )
+
+
 def solution(mesh):
+    program = functools.partial(block_body, mesh) if fits(mesh) else body
     return jax.shard_map(
-        body,
+        program,
         mesh=mesh,
         in_specs=(
             P(None, ("dp", "tensor"), None),

time: 1070 us -> 461 us (0.43)
  waiting for transfers between devices: 742 us -> 0.03 us
  Pallas kernels: 0 us -> 172 us
  matrix products: 154 us -> 125 us
  blocking collectives: 74 us -> 48.3 us
  local copies, waits for them, and re-layouts: 16.2 us -> 39.7 us
  between operations: 17.1 us -> 1.88 us
  other arithmetic: 54 us -> 64.8 us
    reduce_scatter x11 -> x0, waiting for transfers between devices: 512 us -> none  [the longest x4 225 us: collect_rows(): lax.psum_scatter(jnp.dot(operand, weight, preferred_element_type=jnp.floa...]
    all_gather x10 -> x0, waiting for transfers between devices: 227 us -> none  [the longest x4 120 us: spread_grad(): return lax.all_gather(block_rows, 'tensor', axis=0, tiled=True)]
    pallas_call x0 -> x2, Pallas kernels: none -> 172 us  [the longest x1 87.8 us: scatter_all(): pl.pallas_call(functools.partial(scatter_kernel, depth, bit_count, shard)...]
    dot_general x22 -> x11, matrix products: 86.4 us -> 61.7 us  [the longest x1 18.6 us: block_body(): jnp.einsum('rd,hdn->hrn', second_input, up_weight, preferred_element_type...]
    all_gather x3 -> x1, blocking collectives: 34.2 us -> 10.9 us  [block_body(): gains = lax.all_gather(ln_gain[0], 'dp', axis=1, tiled=True).astype(F32)]
    convert_element_type x5 -> x10, other arithmetic: 6.81 us -> 29.6 us  [the longest x1 13.4 us: block_body(): activated = gelu_exact(hidden_pre).astype(BF16)]
  transfers between devices with their start and end apart: 22 -> 10, of which waited for: 20 -> 0; matrix products, arithmetic and copies ran while one was open for 17% -> 9% of each run, Pallas kernels for 0% -> 0%
where the time goes in v1:
time: 461 us; the launch traced here: 454 us
  Pallas kernels  172 us (37%)
  matrix products  125 us (27%)
  other arithmetic  64.8 us (14%)
  blocking collectives  48.3 us (10%)
  local copies, waits for them, and re-layouts  39.7 us (9%)
    pallas_call x1, Pallas kernels, scatter_all(): pl.pallas_call(functools.partial(scatter_kernel, depth, bit_count, shard)...  87.8 us
    pallas_call x1, Pallas kernels, gather_all(): pl.pallas_call(functools.partial(gather_kernel, depth, bit_count, shard),...  83.8 us
    unnamed x1, blocking collectives  37.4 us
    dot_general x1, matrix products, block_body(): jnp.einsum('rd,hdn->hrn', second_input, up_weight, preferred_element_type...  18.6 us
    convert_element_type x1, other arithmetic, attend_back(): grad_scores = (probability * (grad_prob - inner_sum)).astype(jnp.bfloat16)  17 us
    dot_general x1, matrix products, attend_back(): jnp.einsum('qhd,khd->hqk', grad_mix, value_rows, preferred_element_type=j...  16.8 us
    unnamed x88, local copies, waits for them, and re-layouts  15.5 us
    sub x1, matrix products, attend_back(): probability = jnp.exp(scores - highest) / totals  15.4 us
  transfers between devices with their start and end apart: 10, of which 0 were waited for; matrix products, arithmetic and copies ran while one was open for 9% of the time, Pallas kernels for 0%

profile of v1, /device:TPU:1, one launch (start us, length us, event | category | flops | bytes accessed | tf_op | source)
XLA Modules:
  0.0 454.2 jit_solution(15077366560051099270)
XLA Ops:
  0.7 0.9 copy.148
  1.6 1.1 copy.147
  2.8 0.8 copy.150
  3.6 10.9 %all-gather = bf16[1,2,768]{1,0,2:T(2,128)(2,1)S(1)} all-gather(bf16[1,2,96]{1,0,2:T(2,128)(2,1)S(1)} %copy.150), channel_id=2, replica_groups=mesh['dp'=8,'tensor'=4] {'dp'}, dimensions={2}, use_global_device_ids=true | all-gather | bytes 3456 | tf_op jit(solution)/shard_map/all_gather | solution.py:467
  14.9 4.5 %slice_reduce_fusion = (f32[768]{0:T(1024)S(1)}, f32[768]{0:T(1024)S(1)}) fusion(f32[1,2,768]{1,0,2:T(1,128)S(1)} %convert_element_type.191), kind=kLoop, calls=%fused_computation.184 | loop fusion | bytes 12288 | tf_op jit(solution)/shard_map/slice | solution.py:468
  19.6 1.0 pad_maximum_fusion.4.packed
  20.6 1.1 copy-done.3
  21.8 1.1 copy-done.4
  22.9 83.8 %gather_all.1 = (bf16[2,256,768]{2,1,0:T(8,128)(2,1)S(1)}, bf16[2,256,768]{2,1,0:T(8,128)(2,1)S(1)}, bf16[3,2,768,768]{3,2,1,0:T(8,128)(2,1)S(1)}) custom-call(bf16[2,256,768]{2,1,0:T(8,128)(2,1)S(1)} %copy-done.3, bf16[2,256,768]{2,1,0:T(8,128)(2,1)S(1)} %copy-done.4, bf16[3,96,768]{2,1,0:T(8,128)(2,1)S(1)} %pad_maximum_fusion.4.packed), custom_call_target="tpu_custom_call" | custom-call | tf_op jit(solution)/shard_map/gather_all/pallas_call | solution.py:210
  106.7 2.9 copy-done.2
  111.2 3.2 slice_bitcast_fusion
  114.7 1.5 fusion.54
  116.2 1.6 broadcast_select_fusion.7
  117.9 4.5 convolution_convert_fusion
  122.4 1.7 copy.152
  124.2 15.4 %fusion.161 = (f32[6,1024]{1,0:T(8,128)S(1)}, f32[6,1024,1024]{1,2,0:T(8,128)}) fusion(pred[1024,1024]{0,1:T(8,128)(4,1)S(1)} %fusion.54, bf16[1024,3,6,64]{0,3,2,1:T(8,128)(2,1)} %bitcast.441), kind=kOutput, calls=%fused_computation.224 | convolution fusion | flops 830473216 | bytes 27811840 | tf_op jit(solution)/shard_map/sub | solution.py:417
  139.5 10.7 %fusion.122 = bf16[6,64,1024]{2,1,0:T(8,128)(2,1)S(1)} fusion(bf16[1024,3,6,64]{0,3,2,1:T(8,128)(2,1)} %bitcast.442, f32[6,1024,1024]{1,2,0:T(8,128)} %get-tuple-element.89, f32[6,1024]{1,0:T(8,128)S(1)} %get-tuple-element.88), kind=kOutput, calls=%fused_computation.158 | convolution fusion | flops 818282496 | bytes 26763264 | tf_op jit(solution)/shard_map/hqk,khd->qhd/dot_general | solution.py:410
  150.3 0.6 convert_element_type.156
  150.9 2.4 convolution_bitcast_fusion
  153.3 1.1 fusion.132
  155.6 1.5 slice.66
  157.1 1.1 copy.159
  158.2 1.7 fusion.159
  160.7 1.4 broadcast_select_fusion.3
  162.1 7.6 %fusion.73 = f32[2,768,1024]{2,1,0:T(8,128)} fusion(bf16[3,2,768,768]{3,2,1,0:T(8,128)(2,1)} %copy-done.2, bf16[512,768]{1,0:T(8,128)(2,1)S(1)} %get-tuple-element.79, bf16[512,768]{1,0:T(8,128)(2,1)S(1)} %get-tuple-element.78), kind=kOutput, calls=%fused_computation.96 | convolution fusion | flops 2419064832 | bytes 10223616 | tf_op jit(solution)/shard_map/rd,hdn->hrn/dot_general | solution.py:513
  170.2 18.6 %fusion.6 = (f32[2,1024,768]{1,2,0:T(8,128)}, f32[2,768,1024]{2,1,0:T(8,128)S(1)}) fusion(bf16[512,768]{1,0:T(8,128)(2,1)S(1)} %get-tuple-element.81, bf16[512,768]{1,0:T(8,128)(2,1)S(1)} %get-tuple-element.80, bf16[3,2,768,768]{3,2,1,0:T(8,128)(2,1)S(1)} %bitcast.439), kind=kOutput, calls=%fused_computation.14 | convolution fusion | flops 2516582400 | bytes 16515072 | tf_op jit(solution)/shard_map/rd,hdn->hrn/dot_general | solution.py:504
  188.8 13.4 %fusion.24 = (bf16[1024,2,768]{0,2,1:T(8,128)(2,1)S(1)}, f32[1024,2,768]{0,2,1:T(8,128)S(1)}) fusion(f32[2,768,1024]{2,1,0:T(8,128)S(1)} %get-tuple-element.91), kind=kLoop, calls=%fused_computation.46 | loop fusion | flops 102236160 | bytes 15728640 | tf_op jit(solution)/shard_map/convert_element_type | solution.py:505
  202.2 5.8 %fusion.22 = bf16[1024,2,768]{0,2,1:T(8,128)(2,1)} fusion(f32[2,768,1024]{2,1,0:T(8,128)} %fusion.73, f32[1024,2,768]{0,2,1:T(8,128)S(1)} %get-tuple-element.70, f32[2,768,1024]{2,1,0:T(8,128)S(1)} %get-tuple-element.91), kind=kLoop, calls=%fused_computation.43 | loop fusion | flops 22020096 | bytes 22020096 | tf_op jit(solution)/shard_map/convert_element_type | solution.py:515
  208.0 4.6 %fusion.91 = f32[2,512,768]{2,1,0:T(8,128)S(1)} fusion(bf16[3,2,768,768]{3,2,1,0:T(8,128)(2,1)S(1)} %bitcast.439, bf16[2,96,2,8,512]{4,3,2,1,0:T(8,128)(2,1)} %bitcast.454), kind=kOutput, calls=%fused_computation.110 | convolution fusion | flops 2415919104 | bytes 8650752 | tf_op jit(solution)/shard_map/hrn,hdn->rd/dot_general | solution.py:518
  212.6 1.0 fusion.133
  214.0 2.7 fusion.96
  216.7 1.6 copy-done.13
  218.3 1.0 fusion.134
  219.4 8.4 %convert_bitcast_fusion.1 = bf16[1,2,768,768]{3,2,1,0:T(8,128)(2,1)} fusion(f32[2,768,1024]{2,1,0:T(8,128)} %fusion.73, f32[2,1024,768]{1,2,0:T(8,128)S(1)} %bitcast.447, f32[2,768,1024]{2,1,0:T(8,128)S(1)} %get-tuple-element.91, bf16[512,768]{1,0:T(8,128)(2,1)} %copy-done.22, bf16[512,768]{1,0:T(8,128)(2,1)} %copy-done.21), kind=kOutput, calls=%fused_computation.101 | convolution fusion | flops 2442264576 | bytes 22806528 | tf_op jit(solution)/shard_map/rd,hrn->hdn/dot_general | solution.py:516
  227.9 3.8 multiply_reduce_fusion.1
  231.7 3.0 fusion.158
  235.1 4.3 convert_bitcast_fusion
  239.6 0.8 fusion.131
  240.7 11.2 %fusion.125 = bf16[6,64,1024]{2,1,0:T(8,128)(2,1)} fusion(bf16[1024,6,64]{0,2,1:T(8,128)(2,1)S(1)} %bitcast.463, f32[6,1024,1024]{1,2,0:T(8,128)} %get-tuple-element.89, f32[6,1024]{1,0:T(8,128)S(1)} %get-tuple-element.88), kind=kOutput, calls=%fused_computation.159 | convolution fusion | flops 818282496 | bytes 26763264 | tf_op jit(solution)/shard_map/hqk,qhd->khd/dot_general | solution.py:420
  251.8 16.8 %multiply_reduce_fusion = (f32[6,1024]{1,0:T(8,128)S(1)}, f32[6,1024,1024]{1,2,0:T(8,128)}) fusion(f32[6,1024,1024]{1,2,0:T(8,128)} %get-tuple-element.89, f32[6,1024]{1,0:T(8,128)S(1)} %get-tuple-element.88, bf16[1024,6,64]{0,2,1:T(8,128)(2,1)S(1)} %bitcast.464, bf16[1024,3,6,64]{0,3,2,1:T(8,128)(2,1)} %bitcast.443), kind=kOutput, calls=%fused_computation.2 | convolution fusion | flops 824174592 | bytes 51953664 | tf_op jit(solution)/shard_map/qhd,khd->hqk/dot_general | solution.py:419
  268.6 17.0 %multiply_convert_fusion = bf16[6,1024,1024]{1,2,0:T(8,128)(2,1)S(1)} fusion(f32[6,1024,1024]{1,2,0:T(8,128)} %get-tuple-element.93, f32[6,1024]{1,0:T(8,128)S(1)} %get-tuple-element.92, f32[6,1024,1024]{1,2,0:T(8,128)} %get-tuple-element.89, f32[6,1024]{1,0:T(8,128)S(1)} %get-tuple-element.88), kind=kLoop, calls=%fused_computation.1 | loop fusion | flops 25165824 | bytes 62963712 | tf_op jit(solution)/shard_map/convert_element_type | solution.py:422
  285.6 5.1 %multiply_convert_fusion.1 = bf16[6,64,1024]{2,1,0:T(8,128)(2,1)S(1)} fusion(bf16[6,1024,1024]{1,2,0:T(8,128)(2,1)S(1)} %multiply_convert_fusion, bf16[1024,3,6,64]{0,3,2,1:T(8,128)(2,1)} %bitcast.444), kind=kOutput, calls=%fused_computation.149 | convolution fusion | flops 806092800 | bytes 14155776 | tf_op jit(solution)/shard_map/hqk,qhd->khd/dot_general | solution.py:428
  290.7 3.6 multiply_convert_fusion.2
  294.3 0.8 fusion.128
  295.1 1.2 copy.165
  296.9 1.4 copy-done.12
  298.4 3.2 convolution_convert_fusion.1
  301.6 2.7 copy.164
  304.4 4.7 %fusion.86 = f32[2,512,768]{2,1,0:T(8,128)S(1)} fusion(bf16[2,72,2,8,512]{4,3,2,1,0:T(8,128)(2,1)} %bitcast.456, bf16[2,768,768]{2,1,0:T(8,128)(2,1)} %slice_bitcast_fusion), kind=kOutput, calls=%fused_computation.109 | convolution fusion | flops 1811939328 | bytes 7471104 | tf_op jit(solution)/shard_map/hrn,hdn->rd/dot_general | solution.py:535
  309.8 0.9 copy-done.6
  310.7 0.7 copy-done.11
  311.4 3.7 pad_maximum_fusion.grads
  315.2 0.8 fusion.121
  316.0 1.6 fusion.120
  317.5 87.8 %scatter_all.1 = (f32[3,96,768]{2,1,0:T(8,128)}, bf16[2,256,768]{2,1,0:T(8,128)(2,1)}, bf16[2,256,768]{2,1,0:T(8,128)(2,1)}) custom-call(bf16[3,2,768,768]{3,2,1,0:T(8,128)(2,1)} %pad_maximum_fusion.grads, bf16[2,256,768]{2,1,0:T(8,128)(2,1)} %bitcast.448, bf16[2,256,768]{2,1,0:T(8,128)(2,1)} %bitcast.449), custom_call_target="tpu_custom_call" | custom-call | tf_op jit(solution)/shard_map/scatter_all/pallas_call | solution.py:341
  405.3 1.0 slice.55
  406.3 1.0 slice_bitcast_fusion.19
  407.3 1.9 slice_bitcast_fusion.18
  409.2 2.4 convert_element_type.188
  411.5 2.4 convert_element_type.189
  413.9 37.4 %all-reduce = f32[1536]{0:T(1024)S(1)} all-reduce(f32[1536]{0:T(1024)S(1)} %pad_maximum_fusion.5), channel_id=3, replica_groups=mesh['dp'=8,'tensor'=4] {'dp','tensor'}, use_global_device_ids=true, to_apply=%region_15.16.clone | all-reduce | flops 1536 | bytes 12288
  451.5 0.9 copy.172
  452.4 0.7 copy.173
  453.1 0.6 dynamic-slice.1
  (125 shorter events, 7.9 us)
Async XLA Ops:
  0.6 110.0 %copy-start.35 = (s32[2,1,4]{2,1,0:T(1,128)S(1)}, s32[2,1,4]{2,1,0:T(1,128)}, u32[]{:S(2)}) copy-start(s32[2,1,4]{2,1,0:T(1,128)} %param.11) | copy-start | bytes 100
  0.6 110.5 %copy-start.34 = (s32[2,1024]{1,0:T(2,128)S(1)}, s32[2,1024]{1,0:T(2,128)}, u32[]{:S(2)}) copy-start(s32[2,1024]{1,0:T(2,128)} %param.12) | copy-start | bytes 24580
  19.5 98.4 %copy-start.28 = (f32[768]{0:T(1024)}, f32[768]{0:T(1024)S(1)}, u32[]{:S(2)}) copy-start(f32[768]{0:T(1024)S(1)} %get-tuple-element.68) | copy-start | bytes 9220
  20.6 1.1 copy-start.3
  21.8 1.1 copy-start.4
  106.7 2.9 copy-start.2
  109.6 48.6 %copy-start = (bf16[2,256,768]{2,1,0:T(8,128)(2,1)}, bf16[2,256,768]{2,1,0:T(8,128)(2,1)S(1)}, u32[]{:S(2)}) copy-start(bf16[2,256,768]{2,1,0:T(8,128)(2,1)S(1)} %get-tuple-element.14) | copy-start | bytes 2359300
  110.2 12.2 %copy-start.30 = (f32[1,2,2,128]{3,1,2,0:T(2,128)}, f32[1,2,2,128]{3,1,2,0:T(2,128)S(1)}, u32[]{:S(2)}) copy-start(f32[1,2,2,128]{3,1,2,0:T(2,128)S(1)} %copy.195) | copy-start | bytes 6148
  110.2 12.2 %copy-start.32 = (f32[1,2,2,128]{3,1,2,0:T(2,128)}, f32[1,2,2,128]{3,1,2,0:T(2,128)S(1)}, u32[]{:S(2)}) copy-start(f32[1,2,2,128]{3,1,2,0:T(2,128)S(1)} %copy.194) | copy-start | bytes 6148
  110.5 5.7 %collective-permute-start = (bf16[512,768]{1,0:T(8,128)(2,1)S(1)}, bf16[512,768]{1,0:T(8,128)(2,1)}, u32[]{:S(2)}, u32[]{:S(2)}) collective-permute-start(bf16[512,768]{1,0:T(8,128)(2,1)S(1)} %fusion.115), channel_id=1, source_target_pairs={{0,4},{4,0},{8,12},{12,8},{16,20},{20,16},{24,28},{28,24},{1,5},{5... | collective-permute-start | bytes 2359304 | tf_op jit(solution)/shard_map/ppermute | solution.py:442
  110.6 3.8 collective-permute-start.1
  111.1 3.6 collective-permute-start.2
  117.9 6.3 %copy-start.17 = (bf16[512,768]{1,0:T(8,128)(2,1)}, bf16[512,768]{1,0:T(8,128)(2,1)S(1)}, u32[]{:S(2)}) copy-start(bf16[512,768]{1,0:T(8,128)(2,1)S(1)} %get-tuple-element.82) | copy-start | bytes 2359300
  117.9 6.3 %copy-start.19 = (bf16[512,768]{1,0:T(8,128)(2,1)}, bf16[512,768]{1,0:T(8,128)(2,1)S(1)}, u32[]{:S(2)}) copy-start(bf16[512,768]{1,0:T(8,128)(2,1)S(1)} %get-tuple-element.83) | copy-start | bytes 2359300
  150.3 3.0 copy-start.15
  153.3 1.9 copy-start.5
  154.4 3.8 collective-permute-start.3
  155.2 5.5 %collective-permute-start.5 = (bf16[512,768]{1,0:T(8,128)(2,1)S(1)}, bf16[512,768]{1,0:T(8,128)(2,1)}, u32[]{:S(2)}, u32[]{:S(2)}) collective-permute-start(bf16[512,768]{1,0:T(8,128)(2,1)S(1)} %bitcast.437), channel_id=1, source_target_pairs={{0,4},{4,0},{8,12},{12,8},{16,20},{20,16},{24,28},{28,24},{1,5},{5... | collective-permute-start | bytes 2359304 | tf_op jit(solution)/shard_map/ppermute | solution.py:442
  160.5 9.1 %collective-permute-start.4 = (bf16[512,768]{1,0:T(8,128)(2,1)S(1)}, bf16[512,768]{1,0:T(8,128)(2,1)S(1)}, u32[]{:S(2)}, u32[]{:S(2)}) collective-permute-start(bf16[512,768]{1,0:T(8,128)(2,1)S(1)} %multiply_convert_fusion.3), channel_id=1, source_target_pairs={{0,4},{4,0},{8,12},{12,8},{16,20},{20,16},{24,28},{28,24},{1,5},{5... | collective-permute-start | bytes 2359304 | tf_op jit(solution)/shard_map/ppermute | solution.py:442
  160.7 9.5 %slice-start = ((s8[7077888]{0:T(1024)(128)(4,1)}), s8[4194304]{0:T(1024)(128)(4,1)S(1)}, s32[]{:S(2)}) async-start(s8[7077888]{0:T(1024)(128)(4,1)} %bitcast.438), calls=%async_computation | async-start | bytes 8388608
  162.1 7.6 %copy-start.8 = (bf16[512,768]{1,0:T(8,128)(2,1)}, bf16[512,768]{1,0:T(8,128)(2,1)S(1)}, u32[]{:S(2)}) copy-start(bf16[512,768]{1,0:T(8,128)(2,1)S(1)} %get-tuple-element.79) | copy-start | bytes 2359300
  162.1 8.1 %slice-start.1 = ((s8[7077888]{0:T(1024)(128)(4,1)}), s8[2883584]{0:T(1024)(128)(4,1)S(1)}, s32[]{:S(2)}) async-start(s8[7077888]{0:T(1024)(128)(4,1)} %bitcast.438), calls=%async_computation.1 | async-start | bytes 5767168
  170.1 18.6 %copy-start.21 = (bf16[512,768]{1,0:T(8,128)(2,1)}, bf16[512,768]{1,0:T(8,128)(2,1)S(1)}, u32[]{:S(2)}) copy-start(bf16[512,768]{1,0:T(8,128)(2,1)S(1)} %get-tuple-element.80) | copy-start | bytes 2359300
  170.1 18.6 %copy-start.22 = (bf16[512,768]{1,0:T(8,128)(2,1)}, bf16[512,768]{1,0:T(8,128)(2,1)S(1)}, u32[]{:S(2)}) copy-start(bf16[512,768]{1,0:T(8,128)(2,1)S(1)} %get-tuple-element.81) | copy-start | bytes 2359300
  212.6 6.8 %slice-start.2 = ((s8[6291456]{0:T(1024)(128)(4,1)}), s8[4194304]{0:T(1024)(128)(4,1)S(1)}, s32[]{:S(2)}) async-start(s8[6291456]{0:T(1024)(128)(4,1)} %bitcast.446), calls=%async_computation.2 | async-start | bytes 8388608
  213.6 14.3 %collective-permute-start.6 = (bf16[512,768]{1,0:T(8,128)(2,1)}, bf16[512,768]{1,0:T(8,128)(2,1)}, u32[]{:S(2)}, u32[]{:S(2)}) collective-permute-start(bf16[512,768]{1,0:T(8,128)(2,1)} %fusion.133), channel_id=1, source_target_pairs={{0,4},{4,0},{8,12},{12,8},{16,20},{20,16},{24,28},{28,24},{1,5},{5... | collective-permute-start | bytes 2359304 | tf_op jit(solution)/shard_map/ppermute | solution.py:442
  214.0 5.4 %slice-start.3 = ((s8[6291456]{0:T(1024)(128)(4,1)}), s8[2097152]{0:T(1024)(128)(4,1)S(1)}, s32[]{:S(2)}) async-start(s8[6291456]{0:T(1024)(128)(4,1)} %bitcast.446), calls=%async_computation.3 | async-start | bytes 4194304
  216.7 1.6 copy-start.13
  219.3 8.6 %collective-permute-start.8 = (bf16[512,768]{1,0:T(8,128)(2,1)}, bf16[512,768]{1,0:T(8,128)(2,1)}, u32[]{:S(2)}, u32[]{:S(2)}) collective-permute-start(bf16[512,768]{1,0:T(8,128)(2,1)} %fusion.134), channel_id=1, source_target_pairs={{0,4},{4,0},{8,12},{12,8},{16,20},{20,16},{24,28},{28,24},{1,5},{5... | collective-permute-start | bytes 2359304 | tf_op jit(solution)/shard_map/ppermute | solution.py:442
  227.9 7.2 %copy-start.9 = (bf16[512,768]{1,0:T(8,128)(2,1)S(1)}, bf16[512,768]{1,0:T(8,128)(2,1)}, u32[]{:S(2)}) copy-start(bf16[512,768]{1,0:T(8,128)(2,1)} %copy-done.8) | copy-start | bytes 2359300
  234.7 4.9 %copy-start.27 = (bf16[2,768,192]{1,2,0:T(8,128)(2,1)S(1)}, bf16[2,768,192]{1,2,0:T(8,128)(2,1)}, u32[]{:S(2)}) copy-start(bf16[2,768,192]{1,2,0:T(8,128)(2,1)} %copy.159) | copy-start | bytes 1769476
  234.7 4.7 %collective-permute-start.7 = (bf16[512,768]{1,0:T(8,128)(2,1)S(1)}, bf16[512,768]{1,0:T(8,128)(2,1)S(1)}, u32[]{:S(2)}, u32[]{:S(2)}) collective-permute-start(bf16[512,768]{1,0:T(8,128)(2,1)S(1)} %get-tuple-element.71), channel_id=1, source_target_pairs={{0,4},{4,0},{8,12},{12,8},{16,20},{20,16},{24,28},{28,24},{1,5},{5... | collective-permute-start | bytes 2359304 | tf_op jit(solution)/shard_map/ppermute | solution.py:442
  239.5 0.9 copy-start.23
  239.5 1.1 copy-start.25
  290.7 3.6 copy-start.16
  290.7 3.6 copy-start.24
  290.7 3.6 copy-start.26
  294.3 2.0 copy-start.14
  296.3 2.1 copy-start.18
  296.3 2.1 copy-start.20
  296.9 1.4 copy-start.12
  304.3 4.9 %copy-start.10 = (bf16[2,192,768]{1,2,0:T(8,128)(2,1)S(1)}, bf16[2,192,768]{1,2,0:T(8,128)(2,1)}, u32[]{:S(2)}) copy-start(bf16[2,192,768]{1,2,0:T(8,128)(2,1)} %copy.165) | copy-start | bytes 1769476
  309.0 1.7 copy-start.6
  309.0 2.4 copy-start.11
  309.1 6.0 %collective-permute-start.9 = (bf16[512,768]{1,0:T(8,128)(2,1)S(1)}, bf16[512,768]{1,0:T(8,128)(2,1)S(1)}, u32[]{:S(2)}, u32[]{:S(2)}) collective-permute-start(bf16[512,768]{1,0:T(8,128)(2,1)S(1)} %fusion.135), channel_id=1, source_target_pairs={{0,4},{4,0},{8,12},{12,8},{16,20},{20,16},{24,28},{28,24},{1,5},{5... | collective-permute-start | bytes 2359304 | tf_op jit(solution)/shard_map/ppermute | solution.py:442
  311.4 3.7 copy-start.1
  311.4 3.7 copy-start.29
  311.4 3.7 copy-start.31
  311.4 3.8 copy-start.33
  311.4 4.6 %copy-start.7 = (f32[512,768]{1,0:T(8,128)S(1)}, f32[512,768]{1,0:T(8,128)}, u32[]{:S(2)}) copy-start(f32[512,768]{1,0:T(8,128)} %get-tuple-element.72) | copy-start | bytes 4718596

commit v2 on v0

--- a/solution.py
+++ b/solution.py
@@ -1,14 +1,60 @@
+import functools
+
 import jax
 import jax.numpy as jnp
 from jax import lax
+from jax.experimental import pallas as pl
+from jax.experimental.pallas import tpu as pltpu
 from jax.sharding import PartitionSpec as P
 
 D = 768
 HD = 64
-
-
 NEGATIVE = -1e30
 EPSILON = 1e-06
+MESH = pl.DeviceIdType.MESH
+F32 = jnp.float32
+BF16 = jnp.bfloat16
+KINDS = 3
+TILE = 256
+SCALE = HD**-0.5
+
+
+def flip(value, bit):
+    size = 1 << bit
+    return value + size * (1 - 2 * ((value // size) % 2))
+
+
+def flip_mask(value, mask):
+    bit = 0
+    while mask >> bit:
+        if (mask >> bit) & 1:
+            value = flip(value, bit)
+        bit += 1
+    return value
+
+
+def submasks(bits):
+    masks = [0]
+    for bit in bits:
+        masks = masks + [mask | (1 << bit) for mask in masks]
+    return masks
+
+
+def color_order(color, bit_count):
+    order = list(range(bit_count))
+    return order if color == 0 else order[::-1]
+
+
+def device(p, c, z):
+    return (2 * p + c, z)
+
+
+def dot(left, right):
+    return jnp.dot(left, right, preferred_element_type=F32)
+
+
+def dot_nt(left, right):
+    return lax.dot_general(left, right, (((1,), (1,)), ((), ())), preferred_element_type=F32)
 
 
 def normalize(row_block):
@@ -24,6 +70,981 @@
     mean_grad = jnp.mean(scaled, axis=-1, keepdims=True)
     second = jnp.mean(scaled * normed, axis=-1, keepdims=True)
     return inverse * (scaled - mean_grad - normed * second)
+
+
+def remote(source, target, send_sem, recv_sem, dest):
+    return pltpu.make_async_remote_copy(
+        source, target, send_sem, recv_sem, device_id=dest, device_id_type=MESH
+    )
+
+
+def wait_bytes(ref, sem):
+    pltpu.make_async_copy(ref, ref, sem).wait()
+
+
+SEMS = (
+    "tok_s",
+    "tok_r",
+    "gain_s",
+    "gain_r",
+    "code_s",
+    "code_l",
+    "code_r",
+    "z_s",
+    "z_r",
+    "rel_s",
+    "x_s",
+    "x_r",
+    "rs_s",
+    "rs_r",
+    "rz_s",
+    "rz_r",
+    "out_s",
+    "out_r",
+    "pa_s",
+    "pa_r",
+    "pr_s",
+    "pr_r",
+    "sum_s",
+    "sum_r",
+    "all_s",
+    "all_r",
+)
+
+
+def layer_kernel(depth, bit_count, shard, rows, *refs):
+    (tok, cot, packed, gain_in, code_in, y_out, dx_out, g_out, gm_out) = refs[:9]
+    (
+        xb,
+        dyb,
+        ab,
+        bnb,
+        wts,
+        wq,
+        qkv,
+        qtz,
+        vt,
+        kt,
+        pt,
+        bias,
+        ott,
+        orow,
+        dorow,
+        mid,
+        gact,
+        dgel,
+        prs,
+        prr,
+        stage,
+        rx,
+        zrx,
+        gbuf,
+        code,
+        gsum,
+        sum_rx,
+        all_rx,
+        delta,
+    ) = refs[9:38]
+    sem = dict(zip(SEMS, refs[38:]))
+    half = depth // 2
+    columns = 1 << bit_count
+    own_rows = rows // 2
+    chunks = own_rows // TILE
+    dp = lax.axis_index("dp")
+    z = lax.axis_index("tensor")
+    c = dp % 2
+    p = dp // 2
+    buddy = device(p, 1 - c, z)
+    mine = pl.multiple_of(own_rows * c, own_rows)
+    theirs = pl.multiple_of(own_rows * (1 - c), own_rows)
+    lane = lax.broadcasted_iota(jnp.int32, (1, 128), 1)
+    low = lane < HD
+
+    def same(to_c, to_z):
+        return jnp.logical_and(to_c == c, to_z == z)
+
+    def shard_rows(column, color):
+        return pl.ds(pl.multiple_of((2 * column + color) * shard, 32), shard)
+
+    def send_or_copy(is_self, source, target, send_sem, recv_sem, dest):
+        @pl.when(is_self)
+        def _():
+            pltpu.make_async_copy(source, target, recv_sem).start()
+
+        @pl.when(jnp.logical_not(is_self))
+        def _():
+            remote(source, target, send_sem, recv_sem, dest).start()
+
+    def wait_send(is_self, source, send_sem):
+        @pl.when(jnp.logical_not(is_self))
+        def _():
+            wait_bytes(source, send_sem)
+
+    column_peers = []
+    for dz in range(depth):
+        for dc in range(2):
+            if dz or dc:
+                column_peers.append((c if dc == 0 else 1 - c, (z + dz) % depth))
+    plane_peers = [flip_mask(p, mask) for mask in range(1, columns)]
+
+    def entry_barrier():
+        barrier = pltpu.get_barrier_semaphore()
+        peers = [device(p, cc, zz) for cc, zz in column_peers]
+        peers += [device(pp, c, z) for pp in plane_peers]
+        peers += [device(pp, 1 - c, z) for pp in plane_peers]
+        for peer in peers:
+            pl.semaphore_signal(barrier, inc=1, device_id=peer, device_id_type=MESH)
+        pl.semaphore_wait(barrier, len(peers))
+
+    def send_small():
+        remote(code_in, code.at[c], sem["code_s"], sem["code_r"], buddy).start()
+        pltpu.make_async_copy(code_in, code.at[c], sem["code_l"]).start()
+        index = 0
+        for pp in [p] + plane_peers:
+            for cc in (c, 1 - c):
+                if index:
+                    remote(
+                        gain_in,
+                        gbuf.at[dp],
+                        sem["gain_s"].at[index],
+                        sem["gain_r"].at[dp],
+                        device(pp, cc, z),
+                    ).start()
+                index += 1
+        pltpu.make_async_copy(gain_in, gbuf.at[dp], sem["gain_r"].at[dp]).start()
+
+    def finish_small():
+        wait_bytes(code_in, sem["code_s"])
+        wait_bytes(code_in, sem["code_l"])
+        wait_bytes(code.at[1 - c], sem["code_r"])
+        for source in range(2 * columns):
+            wait_bytes(gbuf.at[source], sem["gain_r"].at[source])
+        for index in range(1, 2 * columns):
+            wait_bytes(gain_in, sem["gain_s"].at[index])
+        total = gbuf[0]
+        for source in range(1, 2 * columns):
+            total = total + gbuf[source]
+        gbuf[0] = total
+
+    def row_targets():
+        for m in range(2):
+            to_z, to_c = 2 * m + c, z // half
+            yield m, to_c, to_z, same(to_c, to_z)
+
+    def row_target(which, slot):
+        if which == 0:
+            return xb.at[slot]
+        return dyb.at[pl.ds(pl.multiple_of(own_rows * c + TILE * slot, TILE), TILE)]
+
+    def row_landing(which, slot, to_c):
+        if which == 0:
+            return xb.at[slot]
+        return dyb.at[pl.ds(pl.multiple_of(own_rows * to_c + TILE * slot, TILE), TILE)]
+
+    def send_rows(which, array):
+        for m, to_c, to_z, is_self in row_targets():
+            slot = z % half
+            send_or_copy(
+                is_self,
+                array.at[m],
+                row_landing(which, slot, to_c),
+                sem["tok_s"].at[which, m],
+                sem["tok_r"].at[which, slot],
+                device(p, to_c, to_z),
+            )
+
+    def rows_sent(which, array):
+        for m, to_c, to_z, is_self in row_targets():
+            wait_send(is_self, array.at[m], sem["tok_s"].at[which, m])
+
+    def rows_landed(which):
+        for slot in range(half):
+            wait_bytes(row_target(which, slot), sem["tok_r"].at[which, slot])
+
+    def send_back(which, target):
+        for slot in range(half):
+            to_c, to_z = z % 2, half * c + slot
+            send_or_copy(
+                same(to_c, to_z),
+                stage.at[slot],
+                target.at[z // 2],
+                sem["out_s"].at[which, slot],
+                sem["out_r"].at[which, z // 2],
+                device(p, to_c, to_z),
+            )
+
+    def back_sent(which):
+        for slot in range(half):
+            is_self = same(z % 2, half * c + slot)
+            wait_send(is_self, stage.at[slot], sem["out_s"].at[which, slot])
+
+    def back_landed(which, target):
+        for m in range(2):
+            wait_bytes(target.at[m], sem["out_r"].at[which, m])
+
+    last = depth - 1
+
+    def z_targets():
+        for dz in range(depth):
+            to_z = (z + dz) % depth
+            far = jnp.logical_or(
+                jnp.logical_and(z == 0, to_z == last), jnp.logical_and(z == last, to_z == 0)
+            )
+            yield dz, z // half, to_z, far
+
+    def gather_z(k):
+        for dz, to_c, to_z, far in z_targets():
+            source = packed.at[k]
+            target = wts.at[k, z % half, shard_rows(p, c)]
+            recv = sem["z_r"].at[k, c, z % half]
+            if dz == 0:
+                send_or_copy(
+                    to_c == c, source, target, sem["z_s"].at[k, dz], recv, device(p, to_c, to_z)
+                )
+            else:
+
+                @pl.when(jnp.logical_not(far))
+                def _():
+                    remote(
+                        source, target, sem["z_s"].at[k, dz], recv, device(p, to_c, to_z)
+                    ).start()
+
+    def gather_z_sent(k):
+        for dz, to_c, to_z, far in z_targets():
+            skip = to_c == c if dz == 0 else far
+            wait_send(skip, packed.at[k], sem["z_s"].at[k, dz])
+
+    relays = jnp.logical_or(
+        jnp.logical_and(c == 0, z == last - 1), jnp.logical_and(c == 1, z == 1)
+    )
+    relay_slot = (half - 1) * c
+    relay_to = device(p, c, last * (1 - c))
+
+    def relay_block(k, color):
+        return wts.at[k, relay_slot, shard_rows(p, color)]
+
+    def after_z(k):
+        for color in range(2):
+            for slot in range(half):
+                wait_bytes(wts.at[k, slot, shard_rows(p, color)], sem["z_r"].at[k, color, slot])
+        for color in range(2):
+            gather_step(k, color, 0)
+
+        @pl.when(relays)
+        def _():
+            for color in range(2):
+                block = relay_block(k, color)
+                remote(
+                    block,
+                    block,
+                    sem["rel_s"].at[k, color],
+                    sem["z_r"].at[k, color, relay_slot],
+                    relay_to,
+                ).start()
+
+    def gather_step(k, color, s):
+        order = color_order(color, bit_count)
+        for index, mask in enumerate(submasks(order[:s])):
+            block = wts.at[k, :, shard_rows(flip_mask(p, mask), color)]
+            remote(
+                block,
+                block,
+                sem["x_s"].at[k, color, s, index],
+                sem["x_r"].at[k, color, s, index],
+                device(flip(p, order[s]), c, z),
+            ).start()
+
+    def gather_next(k, s):
+        for color in range(2):
+            order = color_order(color, bit_count)
+            for index, mask in enumerate(submasks(order[:s])):
+                landed = flip(flip_mask(p, mask), order[s])
+                wait_bytes(
+                    wts.at[k, :, shard_rows(landed, color)], sem["x_r"].at[k, color, s, index]
+                )
+            if s + 1 < bit_count:
+                gather_step(k, color, s + 1)
+
+    def gather_sent(k):
+        gather_z_sent(k)
+
+        @pl.when(relays)
+        def _():
+            for color in range(2):
+                wait_bytes(relay_block(k, color), sem["rel_s"].at[k, color])
+
+        for color in range(2):
+            order = color_order(color, bit_count)
+            for s in range(bit_count):
+                for index, mask in enumerate(submasks(order[:s])):
+                    block = wts.at[k, :, shard_rows(flip_mask(p, mask), color)]
+                    wait_bytes(block, sem["x_s"].at[k, color, s, index])
+
+    place = {2: 0, 1: 1, 0: 2}
+
+    def rx_slot(k, color, s, index):
+        return rx.at[k, color, (1 << bit_count) - (1 << (bit_count - s)) + index]
+
+    def scatter_order(color):
+        return color_order(color, bit_count)[::-1]
+
+    def scatter_blocks(k, color, s, away):
+        order = scatter_order(color)
+        for index, mask in enumerate(submasks(order[s + 1 :])):
+            column = flip_mask(p, mask)
+            if away:
+                column = flip(column, order[s])
+            yield index, wts.at[place[k], :, shard_rows(column, color)]
+
+    def scatter_step(k, s):
+        for color in range(2):
+            to = device(flip(p, scatter_order(color)[s]), c, z)
+            for index, block in scatter_blocks(k, color, s, True):
+                remote(
+                    block,
+                    rx_slot(k, color, s, index),
+                    sem["rs_s"].at[k, color, s, index],
+                    sem["rs_r"].at[k, color, s, index],
+                    to,
+                ).start()
+
+    def scatter_next(k, s):
+        for color in range(2):
+            for index, block in scatter_blocks(k, color, s, False):
+                got = rx_slot(k, color, s, index)
+                wait_bytes(got, sem["rs_r"].at[k, color, s, index])
+                block[...] = (block[...].astype(F32) + got[...].astype(F32)).astype(BF16)
+        if s + 1 < bit_count:
+            scatter_step(k, s + 1)
+        else:
+            scatter_z(k)
+
+    def scatter_z_blocks(k):
+        for color in range(2):
+            for slot in range(half):
+                to_z = half * c + slot
+                block = wts.at[place[k], slot, shard_rows(p, color)]
+                yield color, slot, to_z, block, same(color, to_z)
+
+    def scatter_z(k):
+        for color, slot, to_z, block, is_self in scatter_z_blocks(k):
+            send_or_copy(
+                is_self,
+                block,
+                zrx.at[k, z],
+                sem["rz_s"].at[k, color, slot],
+                sem["rz_r"].at[k, z],
+                device(p, color, to_z),
+            )
+
+    def scatter_finish(k):
+        for source in range(depth):
+            wait_bytes(zrx.at[k, source], sem["rz_r"].at[k, source])
+        total = zrx[k, 0].astype(F32)
+        for source in range(1, depth):
+            total = total + zrx[k, source].astype(F32)
+        g_out[k] = total
+
+    def scatter_sent(k):
+        for color in range(2):
+            for s in range(bit_count):
+                for index, block in scatter_blocks(k, color, s, True):
+                    wait_bytes(block, sem["rs_s"].at[k, color, s, index])
+        for color, slot, to_z, block, is_self in scatter_z_blocks(k):
+            wait_send(is_self, block, sem["rz_s"].at[k, color, slot])
+
+    def pair_send(index, buffer):
+        own = buffer.at[pl.ds(mine, own_rows)]
+        remote(own, own, sem["pa_s"].at[index], sem["pa_r"].at[index], buddy).start()
+
+    def pair_landed(index, buffer):
+        wait_bytes(buffer.at[pl.ds(theirs, own_rows)], sem["pa_r"].at[index])
+
+    def pair_sent(index, buffer):
+        wait_bytes(buffer.at[pl.ds(mine, own_rows)], sem["pa_s"].at[index])
+
+    def part_send(index):
+        remote(
+            prs.at[index % 2],
+            prr.at[index % 2],
+            sem["pr_s"].at[index],
+            sem["pr_r"].at[index],
+            buddy,
+        ).start()
+
+    def part_landed(index):
+        wait_bytes(prr.at[index % 2], sem["pr_r"].at[index])
+
+    def part_sent(index):
+        wait_bytes(prs.at[index % 2], sem["pr_s"].at[index])
+
+    def each_half(body, second=None):
+        def step(i, carry):
+            if second is not None:
+                pl.when(i == 1)(second)
+            body(pl.multiple_of(jnp.where(i == 0, mine, theirs), own_rows))
+            return carry
+
+        lax.fori_loop(0, 2, step, 0)
+
+    def own_chunks(body):
+        def step(i, carry):
+            body(i, pl.multiple_of(i * TILE, TILE), pl.multiple_of(mine + i * TILE, TILE))
+            return carry
+
+        lax.fori_loop(0, chunks, step, 0)
+
+    entry_barrier()
+    send_small()
+    gather_z(0)
+    gather_z(1)
+    send_rows(0, tok)
+    gather_z(2)
+    send_rows(1, cot)
+
+    for h in range(6):
+        qtz[h, HD * (1 - h % 2) : HD * (1 - h % 2) + HD, :] = jnp.zeros((HD, rows), BF16)
+    gsum[...] = jnp.zeros(gsum.shape, F32)
+    finish_small()
+    gain_first = gbuf[0, 0:1, :]
+    gain_second = gbuf[0, 1:2, :]
+
+    micro = z // 2
+    owner = z % 2
+    query_image = code[owner, pl.ds(micro, 1), :]
+    key_code = code[owner, pl.ds(2 + micro, 1), :]
+    key_columns = jnp.broadcast_to(key_code, (128, rows)).T
+    for block in range(rows // 128):
+        span = slice(128 * block, 128 * block + 128)
+        key = key_columns[span, 0:1]
+        row_id = lax.broadcasted_iota(jnp.int32, (128, rows), 0) + 128 * block
+        col_id = lax.broadcasted_iota(jnp.int32, (128, rows), 1)
+        seen = jnp.logical_or(key == query_image, row_id == col_id)
+        bias[span, :] = jnp.where(seen, 0.0, NEGATIVE).astype(BF16)
+
+    after_z(0)
+    gather_next(0, 0)
+    after_z(1)
+    rows_landed(0)
+
+    def first_norm(i, at, base):
+        normed, _ = normalize(xb[i].astype(F32))
+        ab[pl.ds(base, TILE), :] = (normed * gain_first).astype(BF16)
+
+    own_chunks(first_norm)
+    pair_send(0, ab)
+    for s in range(1, bit_count):
+        gather_next(0, s)
+
+    def roll(value):
+        return pltpu.roll(value, HD, 1)
+
+    for name, offset in (("q", 0), ("k", 384), ("v", 768), ("o", 1152)):
+        tile = {"q": 0, "k": 128, "v": 256, "o": 640}[name]
+        wq[:, offset : offset + 128] = wts[0, 0, :, tile : tile + 128]
+        wq[:, offset + 128 : offset + 256] = wts[0, 1, :, tile : tile + 128]
+        mixed = {"q": 384, "k": 384, "v": 512, "o": 512}[name]
+        one = wts[0, 0, :, mixed : mixed + 128].astype(F32)
+        two = wts[0, 1, :, mixed : mixed + 128].astype(F32)
+        if name in ("q", "v"):
+            both = jnp.where(low, one, roll(two))
+        else:
+            both = jnp.where(low, roll(one), two)
+        wq[:, offset + 256 : offset + 384] = both.astype(BF16)
+
+    def project(base):
+        span = pl.ds(base, own_rows)
+        source = ab[span, :]
+        for part in range(3):
+            result = dot(source, wq[:, 384 * part : 384 * part + 384])
+            if part == 0:
+                result = result * SCALE
+            qkv[span, 384 * part : 384 * part + 384] = result.astype(BF16)
+            turned = result.T.astype(BF16)
+            if part == 0:
+                for h in range(6):
+                    at = HD * (h % 2)
+                    qtz[h, at : at + HD, span] = turned[HD * h : HD * h + HD]
+            elif part == 1:
+                kt[:, span] = turned
+            else:
+                vt[:, span] = turned
+
+    each_half(project, lambda: pair_landed(0, ab))
+
+    def attend(base, hook):
+        span = pl.ds(base, own_rows)
+        for h in range(6):
+            pair = h // 2
+            keys = qkv[:, 384 + 128 * pair : 512 + 128 * pair]
+            scores = dot(keys, qtz[h, :, span]) + bias[:, span].astype(F32)
+            highest = jnp.max(scores, axis=0, keepdims=True)
+            exponent = jnp.exp(scores - highest)
+            total = jnp.sum(exponent, axis=0, keepdims=True)
+            rounded = (exponent * (1.0 / total)).astype(BF16)
+            pt[h, :, span] = rounded
+            mixed = dot(vt[HD * h : HD * h + HD, :], rounded)
+            ott[HD * h : HD * h + HD, span] = mixed.astype(BF16)
+            hook(h)
+        orow[span, :] = ott[:, span].T
+
+    def attend_loop(i, carry):
+        base = pl.multiple_of(jnp.where(i == 0, theirs, mine), own_rows)
+
+        def hook(h):
+            if h == 2:
+
+                @pl.when(i == 0)
+                def _():
+                    gather_next(1, 0)
+
+                @pl.when(i == 1)
+                def _():
+                    after_z(2)
+
+        attend(base, hook)
+        return carry
+
+    lax.fori_loop(0, 2, attend_loop, 0)
+    out_weight = wq[:, 1152:1536]
+    prs[0] = dot_nt(orow[pl.ds(theirs, own_rows), :], out_weight).astype(BF16)
+    part_send(0)
+
+    def own_out(i, at, base):
+        mid[pl.ds(at, TILE), :] = dot_nt(orow[pl.ds(base, TILE), :], wq[:, 1152:1536])
+
+    own_chunks(own_out)
+    part_landed(0)
+
+    def second_norm(i, at, base):
+        here = pl.ds(at, TILE)
+        middle = xb[i].astype(F32) + (mid[here, :] + prr[0, here, :].astype(F32))
+        mid[here, :] = middle
+        normed, _ = normalize(middle)
+        bnb[pl.ds(base, TILE), :] = (normed * gain_second).astype(BF16)
+
+    own_chunks(second_norm)
+    pair_send(1, bnb)
+    for s in range(1, bit_count):
+        gather_next(1, s)
+    gather_next(2, 0)
+
+    def expand(base):
+        def chunk(i, carry):
+            span = pl.ds(pl.multiple_of(base + i * TILE, TILE), TILE)
+            source = bnb[span, :]
+            for j in range(half):
+                pre = dot(source, wts[1, j])
+                cdf = 0.5 * (1.0 + lax.erf(pre * 0.7071067811865476))
+                density = jnp.exp(pre * pre * -0.5) * 0.3989422804014327
+                gact[j, span, :] = (pre * cdf).astype(BF16)
+                dgel[j, span, :] = (cdf + pre * density).astype(BF16)
+            return carry
+
+        lax.fori_loop(0, chunks, chunk, 0)
+
+    each_half(expand, lambda: pair_landed(1, bnb))
+    rows_landed(1)
+    pair_send(2, dyb)
+    gather_sent(0)
+
+    def grad_tiles(source, slot, width_of):
+        def tile(t, carry):
+            at = pl.multiple_of(t * TILE, TILE)
+            turned = source[:, pl.ds(at, TILE)].T
+            width_of(turned, slot, pl.ds(at, TILE))
+            return carry
+
+        lax.fori_loop(0, D // TILE, tile, 0)
+
+    def down_tile(turned, slot, span):
+        for j in range(half):
+            wts[slot, j, span, :] = dot(turned, gact[j]).astype(BF16)
+
+    def up_tile(turned, slot, span):
+        for j in range(half):
+            wts[slot, j, span, :] = dot(turned, dgel[j]).astype(BF16)
+
+    pair_landed(2, dyb)
+    grad_tiles(dyb, place[2], down_tile)
+    scatter_step(2, 0)
+    for s in range(1, bit_count):
+        gather_next(2, s)
+
+    def contract(base, j_refs, weight):
+        total = dot_nt(j_refs[0, pl.ds(base, TILE), :], wts[weight, 0])
+        for j in range(1, half):
+            total = total + dot_nt(j_refs[j, pl.ds(base, TILE), :], wts[weight, j])
+        return total
+
+    def their_chunks(buffer, weight, into):
+        def step(i, carry):
+            base = pl.multiple_of(theirs + i * TILE, TILE)
+            into[pl.ds(pl.multiple_of(i * TILE, TILE), TILE), :] = contract(
+                base, buffer, weight
+            ).astype(BF16)
+            return carry
+
+        lax.fori_loop(0, chunks, step, 0)
+
+    their_chunks(gact, 2, prs.at[1])
+    part_send(1)
+
+    def through_gelu(base):
+        def chunk(i, carry):
+            span = pl.ds(pl.multiple_of(base + i * TILE, TILE), TILE)
+            source = dyb[span, :]
+            for j in range(half):
+                grad_act = dot(source, wts[2, j])
+                dgel[j, span, :] = (grad_act * dgel[j, span, :].astype(F32)).astype(BF16)
+            return carry
+
+        lax.fori_loop(0, chunks, chunk, 0)
+
+    each_half(through_gelu)
+    part_sent(0)
+    their_chunks(dgel, 1, prs.at[0])
+    part_landed(1)
+
+    def layer_rows(i, at, base):
+        here = pl.ds(at, TILE)
+        total = contract(base, gact, 2) + prr[1, here, :].astype(F32)
+        stage[i] = (mid[here, :] + total).astype(BF16)
+
+    own_chunks(layer_rows)
+    part_send(2)
+    send_back(0, y_out)
+    pair_sent(2, dyb)
+    part_landed(2)
+
+    def second_back(i, at, base):
+        here = pl.ds(at, TILE)
+        grad = contract(base, dgel, 1) + prr[0, here, :].astype(F32)
+        normed, inverse = normalize(mid[here, :])
+        gsum[1:2, :] += jnp.sum(grad * normed, axis=0, keepdims=True)
+        down = dyb[pl.ds(base, TILE), :].astype(F32) + norm_back(
+            grad, gain_second, normed, inverse
+        )
+        mid[here, :] = down
+        dyb[pl.ds(base, TILE), :] = down.astype(BF16)
+
+    own_chunks(second_back)
+    pair_send(3, dyb)
+    gather_sent(1)
+    grad_tiles(bnb, place[1], up_tile)
+    scatter_step(1, 0)
+    scatter_next(2, 0)
+
+    def spread_mix(base):
+        span = pl.ds(base, own_rows)
+        result = dot(dyb[span, :], wq[:, 1152:1536])
+        dorow[span, :] = result.astype(BF16)
+        turned = result.T.astype(BF16)
+        for h in range(6):
+            at = HD * (h % 2)
+            piece = turned[HD * h : HD * h + HD]
+            qtz[h, at : at + HD, span] = piece
+            product = piece.astype(F32) * ott[HD * h : HD * h + HD, span].astype(F32)
+            delta[h, :, span] = jnp.sum(product, axis=0, keepdims=True)
+
+    each_half(spread_mix, lambda: pair_landed(3, dyb))
+
+    def attend_back(pair, carry):
+        def tile(offset):
+            return pl.ds(pl.multiple_of(offset + 128 * pair, 128), 128)
+
+        parts = []
+        for hh in range(2):
+            h = 2 * pair + hh
+            grad_values = dot(pt[h], dorow[:, tile(0)])
+            for q in range(rows // own_rows):
+                span = slice(q * own_rows, (q + 1) * own_rows)
+                grad_prob = dot(qkv[:, tile(768)], qtz[h, :, span])
+                chance = pt[h, :, span].astype(F32)
+                pt[h, :, span] = (chance * (grad_prob - delta[h, :, span])).astype(BF16)
+            grad_keys = dot(pt[h], qkv[:, tile(0)])
+            head = pl.ds(pl.multiple_of(HD * h, HD), HD)
+            grad_queries = dot(kt[head, :], pt[h]) * SCALE
+            parts.append((grad_queries, grad_keys, grad_values))
+        qkv[:, tile(768)] = jnp.where(low, parts[0][2], parts[1][2]).astype(BF16)
+        qkv[:, tile(384)] = jnp.where(low, parts[0][1], parts[1][1]).astype(BF16)
+        turned = jnp.concatenate([parts[0][0], parts[1][0]], axis=0).T
+        qkv[:, tile(0)] = turned.astype(BF16)
+
+        @pl.when(pair == 0)
+        def _():
+            for s in range(1, bit_count):
+                scatter_next(2, s)
+
+        @pl.when(pair == 1)
+        def _():
+            scatter_next(1, 0)
+
+        @pl.when(pair == 2)
+        def _():
+            for s in range(1, bit_count):
+                scatter_next(1, s)
+
+        return carry
+
+    lax.fori_loop(0, 3, attend_back, 0)
+
+    gather_sent(2)
+
+    def first_tiles(t, carry):
+        at = pl.multiple_of(t * TILE, TILE)
+        span = pl.ds(at, TILE)
+        slot = place[0]
+        qkv_part = dot(ab[:, span].T, qkv[...])
+        out_part = dot(dyb[:, span].T, orow[...])
+        for i, target in ((0, 0), (1, 128), (2, 256)):
+            for j in range(2):
+                at = 384 * i + 128 * j
+                wts[slot, j, span, target : target + 128] = qkv_part[:, at : at + 128].astype(BF16)
+        for j in range(2):
+            wts[slot, j, span, 640:768] = out_part[:, 128 * j : 128 * j + 128].astype(BF16)
+        mixed_q = qkv_part[:, 256:384]
+        mixed_k = qkv_part[:, 640:768]
+        mixed_v = qkv_part[:, 1024:1152]
+        mixed_o = out_part[:, 256:384]
+        wts[slot, 0, span, 384:512] = jnp.where(low, mixed_q, roll(mixed_k)).astype(BF16)
+        wts[slot, 1, span, 384:512] = jnp.where(low, roll(mixed_q), mixed_k).astype(BF16)
+        wts[slot, 0, span, 512:640] = jnp.where(low, mixed_v, roll(mixed_o)).astype(BF16)
+        wts[slot, 1, span, 512:640] = jnp.where(low, roll(mixed_v), mixed_o).astype(BF16)
+        return carry
+
+    lax.fori_loop(0, D // TILE, first_tiles, 0)
+    scatter_step(0, 0)
+
+    def first_contract(base, size):
+        return dot_nt(qkv[pl.ds(base, size), :], wq[:, 0:1152])
+
+    part_sent(1)
+    prs[1] = first_contract(theirs, own_rows).astype(BF16)
+    part_send(3)
+    back_sent(0)
+    back_landed(0, y_out)
+    part_landed(3)
+
+    def first_back(i, at, base):
+        here = pl.ds(at, TILE)
+        grad = first_contract(base, TILE) + prr[1, here, :].astype(F32)
+        normed, inverse = normalize(xb[i].astype(F32))
+        gsum[0:1, :] += jnp.sum(grad * normed, axis=0, keepdims=True)
+        result = mid[here, :] + norm_back(grad, gain_first, normed, inverse)
+        stage[i] = result.astype(BF16)
+
+    own_chunks(first_back)
+    send_back(1, dx_out)
+
+    me = 2 * z + c
+    for index, (cc, zz) in enumerate(column_peers):
+        remote(
+            gsum,
+            sum_rx.at[me],
+            sem["sum_s"].at[index],
+            sem["sum_r"].at[me],
+            device(p, cc, zz),
+        ).start()
+    pltpu.make_async_copy(gsum, sum_rx.at[me], sem["sum_r"].at[me]).start()
+
+    scatter_next(0, 0)
+    for source in range(2 * depth):
+        wait_bytes(sum_rx.at[source], sem["sum_r"].at[source])
+    for index in range(len(column_peers)):
+        wait_bytes(gsum, sem["sum_s"].at[index])
+    total = sum_rx[0]
+    for source in range(1, 2 * depth):
+        total = total + sum_rx[source]
+    gsum[...] = total
+    for index, pp in enumerate(plane_peers):
+        remote(
+            gsum, all_rx.at[p], sem["all_s"].at[index], sem["all_r"].at[p], device(pp, c, z)
+        ).start()
+    pltpu.make_async_copy(gsum, all_rx.at[p], sem["all_r"].at[p]).start()
+    scatter_finish(2)
+    scatter_finish(1)
+    for source in range(columns):
+        wait_bytes(all_rx.at[source], sem["all_r"].at[source])
+    for index in range(len(plane_peers)):
+        wait_bytes(gsum, sem["all_s"].at[index])
+    total = all_rx[0]
+    for source in range(1, columns):
+        total = total + all_rx[source]
+    gm_out[...] = total
+    for s in range(1, bit_count):
+        scatter_next(0, s)
+    scatter_finish(0)
+
+    back_landed(1, dx_out)
+    back_sent(1)
+    rows_sent(0, tok)
+    rows_sent(1, cot)
+    pair_sent(0, ab)
+    pair_sent(1, bnb)
+    pair_sent(3, dyb)
+    part_sent(2)
+    part_sent(3)
+    for k in range(KINDS):
+        scatter_sent(k)
+
+
+def whole_layer(mesh, tok, cot, packed, gains, codes):
+    depth = mesh.shape["tensor"]
+    bit_count = (mesh.shape["dp"] // 2).bit_length() - 1
+    columns = 1 << bit_count
+    shard = packed.shape[1]
+    half = depth // 2
+    rows = codes.shape[1]
+    own = rows // 2
+    vmem = pl.BlockSpec(memory_space=pltpu.VMEM)
+    hbm = pl.BlockSpec(memory_space=pl.ANY)
+    sem = pltpu.SemaphoreType.DMA
+    blocks = 1 << (bit_count - 1)
+    scratch = [
+        ((half, TILE, D), BF16),
+        ((rows, D), BF16),
+        ((rows, D), BF16),
+        ((rows, D), BF16),
+        ((KINDS, half, D, D), BF16),
+        ((D, 2 * D), BF16),
+        ((rows, 1152), BF16),
+        ((6, 128, rows), BF16),
+        ((384, rows), BF16),
+        ((384, rows), BF16),
+        ((6, rows, rows), BF16),
+        ((rows, rows), BF16),
+        ((384, rows), BF16),
+        ((rows, 384), BF16),
+        ((rows, 384), BF16),
+        ((own, D), F32),
+        ((half, rows, D), BF16),
+        ((half, rows, D), BF16),
+        ((2, own, D), BF16),
+        ((2, own, D), BF16),
+        ((half, TILE, D), BF16),
+        ((KINDS, 2, columns - 1, half, shard, D), BF16),
+        ((KINDS, depth, shard, D), BF16),
+        ((2 * columns, 8, D), F32),
+        ((2,) + codes.shape, F32),
+        ((8, D), F32),
+        ((2 * depth, 8, D), F32),
+        ((columns, 8, D), F32),
+        ((6, 1, rows), F32),
+    ]
+    sems = {
+        "tok_s": (2, 2),
+        "tok_r": (2, half),
+        "gain_s": (2 * columns,),
+        "gain_r": (2 * columns,),
+        "code_s": (),
+        "code_l": (),
+        "code_r": (),
+        "z_s": (KINDS, depth),
+        "z_r": (KINDS, 2, half),
+        "rel_s": (KINDS, 2),
+        "x_s": (KINDS, 2, bit_count, blocks),
+        "x_r": (KINDS, 2, bit_count, blocks),
+        "rs_s": (KINDS, 2, bit_count, blocks),
+        "rs_r": (KINDS, 2, bit_count, blocks),
+        "rz_s": (KINDS, 2, half),
+        "rz_r": (KINDS, depth),
+        "out_s": (2, half),
+        "out_r": (2, 2),
+        "pa_s": (4,),
+        "pa_r": (4,),
+        "pr_s": (4,),
+        "pr_r": (4,),
+        "sum_s": (2 * depth - 1,),
+        "sum_r": (2 * depth,),
+        "all_s": (columns - 1,),
+        "all_r": (columns,),
+    }
+    return pl.pallas_call(
+        functools.partial(layer_kernel, depth, bit_count, shard, rows),
+        out_shape=(
+            jax.ShapeDtypeStruct(tok.shape, BF16),
+            jax.ShapeDtypeStruct(tok.shape, BF16),
+            jax.ShapeDtypeStruct(packed.shape, F32),
+            jax.ShapeDtypeStruct((8, D), F32),
+        ),
+        in_specs=[hbm, hbm, hbm, vmem, vmem],
+        out_specs=(hbm, hbm, vmem, vmem),
+        scratch_shapes=[pltpu.VMEM(shape, dtype) for shape, dtype in scratch]
+        + [sem(sems[name]) for name in SEMS],
+        compiler_params=pltpu.CompilerParams(
+            collective_id=0, has_side_effects=True, vmem_limit_bytes=67043328
+        ),
+        name="whole_layer",
+    )(tok, cot, packed, gains, codes)
+
+
+def block_body(mesh, tokens, cotangent, lengths, padding, ln_gain, w_qkv, w_out, w_up, w_down):
+    depth = mesh.shape["tensor"]
+    dp = lax.axis_index("dp")
+    z = lax.axis_index("tensor")
+    shard = w_up.shape[1]
+    width = w_qkv.shape[3]
+    pair = 2 * HD
+
+    qkv = w_qkv[0]
+    out_t = w_out[0].T
+    packed = jnp.stack(
+        [
+            jnp.concatenate(
+                [
+                    qkv[:, 0, :pair],
+                    qkv[:, 1, :pair],
+                    qkv[:, 2, :pair],
+                    qkv[:, 0, pair:],
+                    qkv[:, 1, pair:],
+                    qkv[:, 2, pair:],
+                    out_t[:, pair:],
+                    out_t[:, :pair],
+                ],
+                axis=1,
+            ),
+            w_up[0],
+            w_down[0].T,
+        ]
+    )
+    gain_rows = jnp.zeros((8, D), F32)
+    gain_rows = lax.dynamic_update_slice(gain_rows, ln_gain[0].astype(F32), (0, dp * shard))
+    places = lax.iota(jnp.int32, padding.shape[1])
+    bounds = jnp.cumsum(lengths[:, 0], axis=1)
+    picture = jnp.sum((places[None, :, None] >= bounds[:, None, :]).astype(jnp.int32), axis=2)
+    key_code = jnp.where(padding == 1, picture, -1)
+    codes = jnp.concatenate([picture, key_code, picture, picture], axis=0).astype(F32)
+
+    y_back, dx_back, summed, gain_sum = whole_layer(
+        mesh, tokens, cotangent, packed, gain_rows, codes
+    )
+    part = 2 * D // (mesh.shape["dp"] * depth)
+    gain_result = lax.dynamic_slice(gain_sum[:2].reshape(-1), ((dp * depth + z) * part,), (part,))
+    first = summed[0]
+    qkv_grad = jnp.stack(
+        [
+            jnp.concatenate(
+                [
+                    first[:, pair * i : pair * i + pair],
+                    first[:, 3 * pair + HD * i : 3 * pair + HD * i + HD],
+                ],
+                axis=1,
+            )
+            for i in range(3)
+        ],
+        axis=1,
+    )[None]
+    out_grad = jnp.concatenate([first[:, 5 * pair :], first[:, 4 * pair + HD : 5 * pair]], axis=1)
+    return (
+        y_back.astype(F32),
+        dx_back.astype(F32),
+        gain_result,
+        qkv_grad,
+        out_grad.T[None],
+        summed[1][None],
+        summed[2].T[None],
+    )
 
 
 def visible(lengths_row, padding_row):
@@ -252,29 +1273,48 @@
     return (layer_out, input_grad, gain_result, qkv_grad, out_grad, up_grad, down_grad)
 
 
+def fits(mesh, tokens, w_qkv):
+    dp_size, depth = mesh.shape["dp"], mesh.shape["tensor"]
+    columns = dp_size // 2
+    return (
+        depth == 4
+        and dp_size >= 4
+        and columns & (columns - 1) == 0
+        and D % (dp_size * 32) == 0
+        and tokens.shape[0] == 2
+        and tokens.shape[1] == dp_size * depth * TILE
+        and w_qkv.shape[0] == 1
+    )
+
+
 def solution(mesh):
-    return jax.shard_map(
-        body,
-        mesh=mesh,
-        in_specs=(
-            P(None, ("dp", "tensor"), None),
-            P(None, ("dp", "tensor"), None),
-            P(None, "dp", None),
-            P(None, "dp"),
-            P(None, None, "dp"),
-            P(None, "dp", None, "tensor"),
-            P(None, "tensor", "dp"),
-            P(None, "dp", "tensor"),
-            P(None, "tensor", "dp"),
-        ),
-        out_specs=(
-            P(None, ("dp", "tensor"), None),
-            P(None, ("dp", "tensor"), None),
-            P(("dp", "tensor")),
-            P(None, "dp", None, "tensor"),
-            P(None, "tensor", "dp"),
-            P(None, "dp", "tensor"),
-            P(None, "tensor", "dp"),
-        ),
-        check_vma=False,
-    )
+    def run(tokens, cotangent, lengths, padding, ln_gain, w_qkv, *rest):
+        one_block = fits(mesh, tokens, w_qkv)
+        program = functools.partial(block_body, mesh) if one_block else body
+        return jax.shard_map(
+            program,
+            mesh=mesh,
+            in_specs=(
+                P(None, ("dp", "tensor"), None),
+                P(None, ("dp", "tensor"), None),
+                P(None, "dp", None),
+                P(None, "dp"),
+                P(None, None, "dp"),
+                P(None, "dp", None, "tensor"),
+                P(None, "tensor", "dp"),
+                P(None, "dp", "tensor"),
+                P(None, "tensor", "dp"),
+            ),
+            out_specs=(
+                P(None, ("dp", "tensor"), None),
+                P(None, ("dp", "tensor"), None),
+                P(("dp", "tensor")),
+                P(None, "dp", None, "tensor"),
+                P(None, "tensor", "dp"),
+                P(None, "dp", "tensor"),
+                P(None, "tensor", "dp"),
+            ),
+            check_vma=False,
+        )(tokens, cotangent, lengths, padding, ln_gain, w_qkv, *rest)
+
+    return run

time: 1070 us -> 220 us (0.21)
  waiting for transfers between devices: 742 us -> 0 us
  Pallas kernels: 0 us -> 202 us
  matrix products: 154 us -> 0 us
  blocking collectives: 74 us -> 0 us
  other arithmetic: 54 us -> 9.15 us
  between operations: 17.1 us -> 0.72 us
    reduce_scatter x11 -> x0, waiting for transfers between devices: 512 us -> none  [the longest x4 225 us: collect_rows(): lax.psum_scatter(jnp.dot(operand, weight, preferred_element_type=jnp.floa...]
    all_gather x10 -> x0, waiting for transfers between devices: 227 us -> none  [the longest x4 120 us: spread_grad(): return lax.all_gather(block_rows, 'tensor', axis=0, tiled=True)]
    pallas_call x0 -> x1, Pallas kernels: none -> 202 us  [whole_layer(): pl.pallas_call(functools.partial(layer_kernel, depth, bit_count, shard, r...]
    dot_general x32 -> x0, matrix products: 132 us -> none  [the longest x2 22 us: body(): jnp.dot(second_input, up_weight, preferred_element_type=jnp.float32)]
    unnamed x1 -> x0, blocking collectives: 39.8 us -> none
    all_gather x3 -> x0, blocking collectives: 34.2 us -> none  [the longest x1 12.9 us: collect_weights(): lax.all_gather(w_qkv[layer_index], 'dp', axis=0, tiled=True)]
    convert_element_type x7 -> x4, other arithmetic: 23.3 us -> 4.93 us  [the longest x1 2.38 us: block_body(): y_back.astype(F32)]
    sub x2 -> x0, matrix products: 17 us -> none  [attend(): exponent = jnp.exp(scores - highest)]
  transfers between devices with their start and end apart: 22 -> 0, of which waited for: 20 -> 0; matrix products, arithmetic and copies ran while one was open for 17% -> 0% of each run, Pallas kernels for 0% -> 0%
where the time goes in v2:
time: 220 us; the launch traced here: 219 us
  Pallas kernels  202 us (92%)
  other arithmetic  9.15 us (4%)
  local copies, waits for them, and re-layouts  7.91 us (4%)
    pallas_call x1, Pallas kernels, whole_layer(): pl.pallas_call(functools.partial(layer_kernel, depth, bit_count, shard, r...  202 us

profile of v2, /device:TPU:1, one launch (start us, length us, event | category | flops | bytes accessed | tf_op | source)
XLA Modules:
  0.0 219.4 jit_solution(7206293110788756637)
XLA Ops:
  0.6 0.9 reduce_window_sum.14
  1.5 0.7 bitcast_convert_fusion
  2.1 0.1 convert_reduce_fusion
  2.2 0.7 compare_select_fusion
  3.0 0.6 add_convert_fusion.refs_4_
  3.6 0.6 broadcast_in_dim.18
  4.2 1.6 dynamic_update_slice.3.refs_3_
  5.8 0.9 copy.18
  6.7 0.8 slice_bitcast_fusion.2
  7.5 0.8 slice_bitcast_fusion.5
  8.3 0.1 concatenate.18
  8.4 1.8 pad_maximum_fusion.refs_2_
  10.2 201.7 %whole_layer.1 = (bf16[2,256,768]{2,1,0:T(8,128)(2,1)}, bf16[2,256,768]{2,1,0:T(8,128)(2,1)}, f32[3,96,768]{2,1,0:T(8,128)}, f32[8,768]{1,0:T(8,128)}) custom-call(bf16[2,256,768]{2,1,0:T(8,128)(2,1)} %refs_0_.1, bf16[2,256,768]{2,1,0:T(8,128)(2,1)} %refs_1_.1, bf16[3,96,768]{2,1,0:T(8,128)(2,1)} %pad_maximum_fusion.refs_2_, ...), custom_call_target="tpu_custom_call" | custom-call | tf_op jit(solution)/shard_map/whole_layer/pallas_call | solution.py:963
  211.9 0.0 copy-start
  211.9 0.8 slice.68
  212.7 0.6 dynamic_slice.3
  213.3 2.4 %convert_element_type.22 = f32[2,256,768]{2,1,0:T(8,128)} convert(bf16[2,256,768]{2,1,0:T(8,128)(2,1)} %get-tuple-element.11) | non-fusion elementwise | flops 393216 | bytes 2359296 | tf_op jit(solution)/shard_map/convert_element_type | solution.py:1040
  215.7 0.0 copy-done
  215.7 0.9 slice_bitcast_fusion
  216.6 0.0 copy-start.1
  216.6 0.1 fusion.1
  216.7 0.7 copy.19
  217.5 0.7 maximum_bitcast_fusion
  218.2 0.0 copy-done.1
  218.2 1.3 convert_element_type.23
  (6 shorter events, 0.1 us)
Async XLA Ops:
  211.9 3.8 %copy-start = (f32[3,96,768]{2,1,0:T(8,128)S(1)}, f32[3,96,768]{2,1,0:T(8,128)}, u32[]{:S(2)}) copy-start(f32[3,96,768]{2,1,0:T(8,128)} %get-tuple-element.14) | copy-start | bytes 2654212
  216.6 1.6 copy-start.1

commit v3 on v2

--- a/solution.py
+++ b/solution.py
@@ -15,6 +15,10 @@
 F32 = jnp.float32
 BF16 = jnp.bfloat16
 KINDS = 3
+HALF = 48
+GATHER = ((0, 0, HALF), (0, HALF, HALF), (1, 0, HALF), (1, HALF, HALF), (2, 0, 2 * HALF))
+SCATTER = ((2, 0, 2 * HALF), (1, 0, 2 * HALF), (0, 0, HALF), (0, HALF, HALF))
+RELAYED = (2, 1, 0)
 TILE = 256
 SCALE = HD**-0.5
 
@@ -88,7 +92,6 @@
     "gain_s",
     "gain_r",
     "code_s",
-    "code_l",
     "code_r",
     "z_s",
     "z_r",
@@ -99,6 +102,7 @@
     "rs_r",
     "rz_s",
     "rz_r",
+    "far_r",
     "out_s",
     "out_r",
     "pa_s",
@@ -113,7 +117,8 @@
 
 
 def layer_kernel(depth, bit_count, shard, rows, *refs):
-    (tok, cot, packed, gain_in, code_in, y_out, dx_out, g_out, gm_out) = refs[:9]
+    (tok, cot, first_in, up_in, down_in, gain_in, pad_in, length_in) = refs[:8]
+    (y_out, dx_out, g_out, gm_out) = refs[8:12]
     (
         xb,
         dyb,
@@ -138,14 +143,16 @@
         stage,
         rx,
         zrx,
+        far_rx,
         gbuf,
+        gains,
         code,
         gsum,
         sum_rx,
         all_rx,
         delta,
-    ) = refs[9:38]
-    sem = dict(zip(SEMS, refs[38:]))
+    ) = refs[12:43]
+    sem = dict(zip(SEMS, refs[43:]))
     half = depth // 2
     columns = 1 << bit_count
     own_rows = rows // 2
@@ -163,9 +170,6 @@
     def same(to_c, to_z):
         return jnp.logical_and(to_c == c, to_z == z)
 
-    def shard_rows(column, color):
-        return pl.ds(pl.multiple_of((2 * column + color) * shard, 32), shard)
-
     def send_or_copy(is_self, source, target, send_sem, recv_sem, dest):
         @pl.when(is_self)
         def _():
@@ -196,35 +200,52 @@
             pl.semaphore_signal(barrier, inc=1, device_id=peer, device_id_type=MESH)
         pl.semaphore_wait(barrier, len(peers))
 
+    def make_small():
+        gbuf[dp] = jnp.zeros(gbuf.shape[1:], F32)
+        gbuf[dp, 0:2, 0:shard] = gain_in[...].astype(F32)
+        places = lax.broadcasted_iota(jnp.int32, (1, rows), 1)
+        for m in range(2):
+            image = jnp.zeros((1, rows), jnp.int32)
+            bound = 0
+            for k in range(length_in.shape[1]):
+                bound = bound + length_in[m, k]
+                image = image + (places >= bound).astype(jnp.int32)
+            key = jnp.where(pad_in[m : m + 1, :] == 1, image, -1)
+            code[c, m : m + 1, :] = image.astype(F32)
+            code[c, 2 + m : 3 + m, :] = key.astype(F32)
+
     def send_small():
-        remote(code_in, code.at[c], sem["code_s"], sem["code_r"], buddy).start()
-        pltpu.make_async_copy(code_in, code.at[c], sem["code_l"]).start()
+        remote(code.at[c], code.at[c], sem["code_s"], sem["code_r"], buddy).start()
         index = 0
         for pp in [p] + plane_peers:
             for cc in (c, 1 - c):
                 if index:
                     remote(
-                        gain_in,
+                        gbuf.at[dp],
                         gbuf.at[dp],
                         sem["gain_s"].at[index],
                         sem["gain_r"].at[dp],
                         device(pp, cc, z),
                     ).start()
                 index += 1
-        pltpu.make_async_copy(gain_in, gbuf.at[dp], sem["gain_r"].at[dp]).start()
 
     def finish_small():
-        wait_bytes(code_in, sem["code_s"])
-        wait_bytes(code_in, sem["code_l"])
+        wait_bytes(code.at[c], sem["code_s"])
         wait_bytes(code.at[1 - c], sem["code_r"])
+        index = 0
+        for pp in [p] + plane_peers:
+            for cc in (c, 1 - c):
+                if index:
+                    wait_bytes(gbuf.at[dp], sem["gain_s"].at[index])
+                    source = 2 * pp + cc
+                    wait_bytes(gbuf.at[source], sem["gain_r"].at[source])
+                index += 1
+        rest = jnp.zeros((8, D - 128), F32)
+        total = jnp.zeros((8, D), F32)
         for source in range(2 * columns):
-            wait_bytes(gbuf.at[source], sem["gain_r"].at[source])
-        for index in range(1, 2 * columns):
-            wait_bytes(gain_in, sem["gain_s"].at[index])
-        total = gbuf[0]
-        for source in range(1, 2 * columns):
-            total = total + gbuf[source]
-        gbuf[0] = total
+            wide = jnp.concatenate([gbuf[source], rest], axis=1)
+            total = total + (pltpu.roll(wide, shard * source, 1) if source else wide)
+        gains[...] = total
 
     def row_targets():
         for m in range(2):
@@ -284,174 +305,260 @@
 
     last = depth - 1
 
+    def two_ends(low_core, high_core):
+        return jnp.logical_or(
+            jnp.logical_and(c == 0, z == low_core), jnp.logical_and(c == 1, z == high_core)
+        )
+
+    ends = two_ends(last, 0)
+    relays = two_ends(last - 1, 1)
+    relay_to = device(p, c, last * (1 - c))
+    relay_from = device(p, c, last - 1 + c * (2 - last))
+
+    def unit_rows(unit, column, color):
+        _, start, size = unit
+        return pl.ds(pl.multiple_of((2 * column + color) * shard + start, 16), size)
+
+    def unit_source(unit):
+        return (first_in, up_in, down_in)[unit[0]].at[pl.ds(unit[1], unit[2])]
+
     def z_targets():
         for dz in range(depth):
             to_z = (z + dz) % depth
-            far = jnp.logical_or(
-                jnp.logical_and(z == 0, to_z == last), jnp.logical_and(z == last, to_z == 0)
-            )
-            yield dz, z // half, to_z, far
-
-    def gather_z(k):
+            yield dz, z // half, to_z, to_z == last * (1 - z // half)
+
+    def gather_z(u):
+        unit = GATHER[u]
         for dz, to_c, to_z, far in z_targets():
-            source = packed.at[k]
-            target = wts.at[k, z % half, shard_rows(p, c)]
-            recv = sem["z_r"].at[k, c, z % half]
+            source = unit_source(unit)
+            target = wts.at[unit[0], z % half, unit_rows(unit, p, c)]
+            recv = sem["z_r"].at[u, c, z % half]
             if dz == 0:
                 send_or_copy(
-                    to_c == c, source, target, sem["z_s"].at[k, dz], recv, device(p, to_c, to_z)
+                    to_c == c, source, target, sem["z_s"].at[u, dz], recv, device(p, to_c, to_z)
                 )
             else:
 
                 @pl.when(jnp.logical_not(far))
                 def _():
                     remote(
-                        source, target, sem["z_s"].at[k, dz], recv, device(p, to_c, to_z)
+                        source, target, sem["z_s"].at[u, dz], recv, device(p, to_c, to_z)
                     ).start()
 
-    def gather_z_sent(k):
+    def gather_z_sent(u):
         for dz, to_c, to_z, far in z_targets():
             skip = to_c == c if dz == 0 else far
-            wait_send(skip, packed.at[k], sem["z_s"].at[k, dz])
-
-    relays = jnp.logical_or(
-        jnp.logical_and(c == 0, z == last - 1), jnp.logical_and(c == 1, z == 1)
-    )
-    relay_slot = (half - 1) * c
-    relay_to = device(p, c, last * (1 - c))
-
-    def relay_block(k, color):
-        return wts.at[k, relay_slot, shard_rows(p, color)]
-
-    def after_z(k):
+            wait_send(skip, unit_source(GATHER[u]), sem["z_s"].at[u, dz])
+
+    def relay_block(u, color, slot):
+        unit = GATHER[u]
+        return wts.at[unit[0], slot, unit_rows(unit, p, color)]
+
+    def after_z(u):
+        unit = GATHER[u]
         for color in range(2):
             for slot in range(half):
-                wait_bytes(wts.at[k, slot, shard_rows(p, color)], sem["z_r"].at[k, color, slot])
-        for color in range(2):
-            gather_step(k, color, 0)
+                wait_bytes(
+                    wts.at[unit[0], slot, unit_rows(unit, p, color)], sem["z_r"].at[u, color, slot]
+                )
 
         @pl.when(relays)
         def _():
             for color in range(2):
-                block = relay_block(k, color)
+                for slot in range(half):
+                    block = relay_block(u, color, slot)
+                    remote(
+                        block,
+                        block,
+                        sem["rel_s"].at[u, color, slot],
+                        sem["z_r"].at[u, color, slot],
+                        relay_to,
+                    ).start()
+
+        gather_step(u, 0)
+
+    def gather_blocks(u, color, s, landed):
+        unit = GATHER[u]
+        order = color_order(color, bit_count)
+        for index, mask in enumerate(submasks(order[:s])):
+            column = flip_mask(p, mask)
+            if landed:
+                column = flip(column, order[s])
+            yield index, wts.at[unit[0], :, unit_rows(unit, column, color)]
+
+    def gather_step(u, s):
+        for color in range(2):
+            to = device(flip(p, color_order(color, bit_count)[s]), c, z)
+            for index, block in gather_blocks(u, color, s, False):
                 remote(
                     block,
                     block,
-                    sem["rel_s"].at[k, color],
-                    sem["z_r"].at[k, color, relay_slot],
-                    relay_to,
+                    sem["x_s"].at[u, color, s, index],
+                    sem["x_r"].at[u, color, s, index],
+                    to,
                 ).start()
 
-    def gather_step(k, color, s):
-        order = color_order(color, bit_count)
-        for index, mask in enumerate(submasks(order[:s])):
-            block = wts.at[k, :, shard_rows(flip_mask(p, mask), color)]
-            remote(
-                block,
-                block,
-                sem["x_s"].at[k, color, s, index],
-                sem["x_r"].at[k, color, s, index],
-                device(flip(p, order[s]), c, z),
-            ).start()
-
-    def gather_next(k, s):
+    def gather_next(u, s):
         for color in range(2):
-            order = color_order(color, bit_count)
-            for index, mask in enumerate(submasks(order[:s])):
-                landed = flip(flip_mask(p, mask), order[s])
-                wait_bytes(
-                    wts.at[k, :, shard_rows(landed, color)], sem["x_r"].at[k, color, s, index]
-                )
-            if s + 1 < bit_count:
-                gather_step(k, color, s + 1)
+            for index, block in gather_blocks(u, color, s, True):
+                wait_bytes(block, sem["x_r"].at[u, color, s, index])
+        if s + 1 < bit_count:
+            gather_step(u, s + 1)
+
+    def gather_last(*units):
+        for u in units:
+            for s in range(1, bit_count):
+                gather_next(u, s)
 
     def gather_sent(k):
-        gather_z_sent(k)
+        for u, unit in enumerate(GATHER):
+            if unit[0] == k:
+                gather_unit_sent(u)
+
+    def gather_unit_sent(u):
+        gather_z_sent(u)
 
         @pl.when(relays)
         def _():
             for color in range(2):
-                wait_bytes(relay_block(k, color), sem["rel_s"].at[k, color])
+                for slot in range(half):
+                    wait_bytes(relay_block(u, color, slot), sem["rel_s"].at[u, color, slot])
 
         for color in range(2):
-            order = color_order(color, bit_count)
             for s in range(bit_count):
-                for index, mask in enumerate(submasks(order[:s])):
-                    block = wts.at[k, :, shard_rows(flip_mask(p, mask), color)]
-                    wait_bytes(block, sem["x_s"].at[k, color, s, index])
+                for index, block in gather_blocks(u, color, s, False):
+                    wait_bytes(block, sem["x_s"].at[u, color, s, index])
 
     place = {2: 0, 1: 1, 0: 2}
 
-    def rx_slot(k, color, s, index):
-        return rx.at[k, color, (1 << bit_count) - (1 << (bit_count - s)) + index]
+    def rx_slot(u, color, s, index):
+        unit = SCATTER[u]
+        slot = (1 << bit_count) - (1 << (bit_count - s)) + index
+        return rx.at[unit[0], color, slot, :, pl.ds(unit[1], unit[2])]
 
     def scatter_order(color):
         return color_order(color, bit_count)[::-1]
 
-    def scatter_blocks(k, color, s, away):
+    def scatter_blocks(u, color, s, away):
+        unit = SCATTER[u]
         order = scatter_order(color)
         for index, mask in enumerate(submasks(order[s + 1 :])):
             column = flip_mask(p, mask)
             if away:
                 column = flip(column, order[s])
-            yield index, wts.at[place[k], :, shard_rows(column, color)]
-
-    def scatter_step(k, s):
+            yield index, wts.at[place[unit[0]], :, unit_rows(unit, column, color)]
+
+    def scatter_step(u, s):
         for color in range(2):
             to = device(flip(p, scatter_order(color)[s]), c, z)
-            for index, block in scatter_blocks(k, color, s, True):
+            for index, block in scatter_blocks(u, color, s, True):
                 remote(
                     block,
-                    rx_slot(k, color, s, index),
-                    sem["rs_s"].at[k, color, s, index],
-                    sem["rs_r"].at[k, color, s, index],
+                    rx_slot(u, color, s, index),
+                    sem["rs_s"].at[u, color, s, index],
+                    sem["rs_r"].at[u, color, s, index],
                     to,
                 ).start()
 
-    def scatter_next(k, s):
+    def scatter_next(u, s):
         for color in range(2):
-            for index, block in scatter_blocks(k, color, s, False):
-                got = rx_slot(k, color, s, index)
-                wait_bytes(got, sem["rs_r"].at[k, color, s, index])
+            for index, block in scatter_blocks(u, color, s, False):
+                got = rx_slot(u, color, s, index)
+                wait_bytes(got, sem["rs_r"].at[u, color, s, index])
                 block[...] = (block[...].astype(F32) + got[...].astype(F32)).astype(BF16)
         if s + 1 < bit_count:
-            scatter_step(k, s + 1)
+            scatter_step(u, s + 1)
         else:
-            scatter_z(k)
-
-    def scatter_z_blocks(k):
+            scatter_z(u)
+
+    def scatter_last(*units):
+        for u in units:
+            for s in range(1, bit_count):
+                scatter_next(u, s)
+
+    def scatter_z_blocks(u):
+        unit = SCATTER[u]
         for color in range(2):
             for slot in range(half):
                 to_z = half * c + slot
-                block = wts.at[place[k], slot, shard_rows(p, color)]
-                yield color, slot, to_z, block, same(color, to_z)
-
-    def scatter_z(k):
-        for color, slot, to_z, block, is_self in scatter_z_blocks(k):
-            send_or_copy(
-                is_self,
-                block,
-                zrx.at[k, z],
-                sem["rz_s"].at[k, color, slot],
-                sem["rz_r"].at[k, z],
-                device(p, color, to_z),
-            )
-
-    def scatter_finish(k):
+                block = wts.at[place[unit[0]], slot, unit_rows(unit, p, color)]
+                yield color, slot, to_z, block
+
+    def summed_on_the_way(u):
+        return SCATTER[u][0] in RELAYED
+
+    def landing(u, source):
+        unit = SCATTER[u]
+        return zrx.at[unit[0], source, pl.ds(unit[1], unit[2])]
+
+    def far_landing(u, color, slot):
+        unit = SCATTER[u]
+        return far_rx.at[unit[0], color, slot, pl.ds(unit[1], unit[2])]
+
+    def scatter_z(u):
+        for color, slot, to_z, block in scatter_z_blocks(u):
+            send, recv = sem["rz_s"].at[u, color, slot], sem["rz_r"].at[u, z]
+            dest = device(p, color, to_z)
+            if not summed_on_the_way(u):
+                send_or_copy(same(color, to_z), block, landing(u, z), send, recv, dest)
+                continue
+
+            @pl.when(jnp.logical_not(jnp.logical_or(ends, relays)))
+            def _():
+                send_or_copy(same(color, to_z), block, landing(u, z), send, recv, dest)
+
+            @pl.when(ends)
+            def _():
+                remote(
+                    block,
+                    far_landing(u, color, slot),
+                    send,
+                    sem["far_r"].at[u, color, slot],
+                    relay_from,
+                ).start()
+
+    def scatter_relay(u):
+        @pl.when(relays)
+        def _():
+            for color, slot, to_z, block in scatter_z_blocks(u):
+                got = far_landing(u, color, slot)
+                wait_bytes(got, sem["far_r"].at[u, color, slot])
+                block[...] = (block[...].astype(F32) + got[...].astype(F32)).astype(BF16)
+                send, recv = sem["rz_s"].at[u, color, slot], sem["rz_r"].at[u, z]
+                dest = device(p, color, to_z)
+                send_or_copy(same(color, to_z), block, landing(u, z), send, recv, dest)
+
+    def scatter_finish(u):
+        unit = SCATTER[u]
         for source in range(depth):
-            wait_bytes(zrx.at[k, source], sem["rz_r"].at[k, source])
-        total = zrx[k, 0].astype(F32)
+            got = functools.partial(wait_bytes, landing(u, source), sem["rz_r"].at[u, source])
+            if summed_on_the_way(u) and source in (0, last):
+                pl.when(z // half != (last - source) // half)(got)
+            else:
+                got()
+        total = landing(u, 0)[...].astype(F32)
         for source in range(1, depth):
-            total = total + zrx[k, source].astype(F32)
-        g_out[k] = total
-
-    def scatter_sent(k):
+            total = total + landing(u, source)[...].astype(F32)
+        g_out[unit[0], unit[1] : unit[1] + unit[2]] = total
+
+    def scatter_sent(u):
         for color in range(2):
             for s in range(bit_count):
-                for index, block in scatter_blocks(k, color, s, True):
-                    wait_bytes(block, sem["rs_s"].at[k, color, s, index])
-        for color, slot, to_z, block, is_self in scatter_z_blocks(k):
-            wait_send(is_self, block, sem["rz_s"].at[k, color, slot])
+                for index, block in scatter_blocks(u, color, s, True):
+                    wait_bytes(block, sem["rs_s"].at[u, color, s, index])
+        for color, slot, to_z, block in scatter_z_blocks(u):
+            local = same(color, to_z)
+            if summed_on_the_way(u):
+                local = jnp.logical_and(local, jnp.logical_not(ends))
+            wait_send(local, block, sem["rz_s"].at[u, color, slot])
+
+    def clear_far():
+        for source in (0, last):
+
+            @pl.when(z // half == (last - source) // half)
+            def _():
+                for k in RELAYED:
+                    zrx[k, source] = jnp.zeros(zrx.shape[2:], BF16)
 
     def pair_send(index, buffer):
         own = buffer.at[pl.ds(mine, own_rows)]
@@ -494,20 +601,23 @@
 
         lax.fori_loop(0, chunks, step, 0)
 
+    make_small()
     entry_barrier()
     send_small()
-    gather_z(0)
-    gather_z(1)
+    for u in range(4):
+        gather_z(u)
     send_rows(0, tok)
-    gather_z(2)
-    send_rows(1, cot)
 
     for h in range(6):
         qtz[h, HD * (1 - h % 2) : HD * (1 - h % 2) + HD, :] = jnp.zeros((HD, rows), BF16)
     gsum[...] = jnp.zeros(gsum.shape, F32)
+    clear_far()
+    after_z(0)
     finish_small()
-    gain_first = gbuf[0, 0:1, :]
-    gain_second = gbuf[0, 1:2, :]
+    gain_first = gains[0:1, :]
+    gain_second = gains[1:2, :]
+    after_z(1)
+    gather_next(0, 0)
 
     micro = z // 2
     owner = z % 2
@@ -522,10 +632,13 @@
         seen = jnp.logical_or(key == query_image, row_id == col_id)
         bias[span, :] = jnp.where(seen, 0.0, NEGATIVE).astype(BF16)
 
-    after_z(0)
-    gather_next(0, 0)
-    after_z(1)
+    after_z(2)
+    gather_next(1, 0)
+    after_z(3)
+    gather_z(4)
+    gather_next(2, 0)
     rows_landed(0)
+    send_rows(1, cot)
 
     def first_norm(i, at, base):
         normed, _ = normalize(xb[i].astype(F32))
@@ -533,8 +646,7 @@
 
     own_chunks(first_norm)
     pair_send(0, ab)
-    for s in range(1, bit_count):
-        gather_next(0, s)
+    gather_last(0, 1)
 
     def roll(value):
         return pltpu.roll(value, HD, 1)
@@ -592,15 +704,23 @@
         base = pl.multiple_of(jnp.where(i == 0, theirs, mine), own_rows)
 
         def hook(h):
-            if h == 2:
+            if h == 1:
 
                 @pl.when(i == 0)
                 def _():
-                    gather_next(1, 0)
+                    gather_next(3, 0)
+
+            if h == 4:
+
+                @pl.when(i == 0)
+                def _():
+                    after_z(4)
+
+            if h == 5:
 
                 @pl.when(i == 1)
                 def _():
-                    after_z(2)
+                    gather_next(4, 0)
 
         attend(base, hook)
         return carry
@@ -625,9 +745,7 @@
 
     own_chunks(second_norm)
     pair_send(1, bnb)
-    for s in range(1, bit_count):
-        gather_next(1, s)
-    gather_next(2, 0)
+    gather_last(2, 3)
 
     def expand(base):
         def chunk(i, carry):
@@ -643,9 +761,9 @@
 
         lax.fori_loop(0, chunks, chunk, 0)
 
-    each_half(expand, lambda: pair_landed(1, bnb))
     rows_landed(1)
     pair_send(2, dyb)
+    each_half(expand, lambda: pair_landed(1, bnb))
     gather_sent(0)
 
     def grad_tiles(source, slot, width_of):
@@ -667,9 +785,8 @@
 
     pair_landed(2, dyb)
     grad_tiles(dyb, place[2], down_tile)
-    scatter_step(2, 0)
-    for s in range(1, bit_count):
-        gather_next(2, s)
+    scatter_step(0, 0)
+    gather_last(4)
 
     def contract(base, j_refs, weight):
         total = dot_nt(j_refs[0, pl.ds(base, TILE), :], wts[weight, 0])
@@ -731,9 +848,9 @@
     own_chunks(second_back)
     pair_send(3, dyb)
     gather_sent(1)
+    scatter_next(0, 0)
     grad_tiles(bnb, place[1], up_tile)
     scatter_step(1, 0)
-    scatter_next(2, 0)
 
     def spread_mix(base):
         span = pl.ds(base, own_rows)
@@ -773,22 +890,22 @@
 
         @pl.when(pair == 0)
         def _():
-            for s in range(1, bit_count):
-                scatter_next(2, s)
-
-        @pl.when(pair == 1)
+            scatter_last(0)
+
+        @pl.when(pair == 2)
         def _():
             scatter_next(1, 0)
 
-        @pl.when(pair == 2)
-        def _():
-            for s in range(1, bit_count):
-                scatter_next(1, s)
-
         return carry
 
     lax.fori_loop(0, 3, attend_back, 0)
 
+    def first_contract(base, size):
+        return dot_nt(qkv[pl.ds(base, size), :], wq[:, 0:1152])
+
+    part_sent(1)
+    prs[1] = first_contract(theirs, own_rows).astype(BF16)
+    part_send(3)
     gather_sent(2)
 
     def first_tiles(t, carry):
@@ -814,16 +931,13 @@
         return carry
 
     lax.fori_loop(0, D // TILE, first_tiles, 0)
-    scatter_step(0, 0)
-
-    def first_contract(base, size):
-        return dot_nt(qkv[pl.ds(base, size), :], wq[:, 0:1152])
-
-    part_sent(1)
-    prs[1] = first_contract(theirs, own_rows).astype(BF16)
-    part_send(3)
+    scatter_step(2, 0)
+    scatter_step(3, 0)
+
     back_sent(0)
     back_landed(0, y_out)
+    scatter_relay(0)
+    scatter_last(1)
     part_landed(3)
 
     def first_back(i, at, base):
@@ -835,7 +949,6 @@
         stage[i] = result.astype(BF16)
 
     own_chunks(first_back)
-    send_back(1, dx_out)
 
     me = 2 * z + c
     for index, (cc, zz) in enumerate(column_peers):
@@ -847,8 +960,12 @@
             device(p, cc, zz),
         ).start()
     pltpu.make_async_copy(gsum, sum_rx.at[me], sem["sum_r"].at[me]).start()
-
-    scatter_next(0, 0)
+    send_back(1, dx_out)
+    scatter_next(2, 0)
+    scatter_next(3, 0)
+    scatter_relay(1)
+    scatter_last(2)
+    scatter_last(3)
     for source in range(2 * depth):
         wait_bytes(sum_rx.at[source], sem["sum_r"].at[source])
     for index in range(len(column_peers)):
@@ -862,8 +979,9 @@
             gsum, all_rx.at[p], sem["all_s"].at[index], sem["all_r"].at[p], device(pp, c, z)
         ).start()
     pltpu.make_async_copy(gsum, all_rx.at[p], sem["all_r"].at[p]).start()
-    scatter_finish(2)
-    scatter_finish(1)
+    scatter_relay(2)
+    scatter_relay(3)
+    scatter_finish(0)
     for source in range(columns):
         wait_bytes(all_rx.at[source], sem["all_r"].at[source])
     for index in range(len(plane_peers)):
@@ -871,10 +989,12 @@
     total = all_rx[0]
     for source in range(1, columns):
         total = total + all_rx[source]
-    gm_out[...] = total
-    for s in range(1, bit_count):
-        scatter_next(0, s)
-    scatter_finish(0)
+    place_of = (2 * D // (2 * columns * depth)) * (dp * depth + z)
+    wanted = jnp.where(place_of < D, total[0:1, :], total[1:2, :])
+    turn = (D - place_of % D) % D
+    gm_out[...] = pltpu.roll(jnp.broadcast_to(wanted, (8, D)), turn, 1)[:, 0:128]
+    for u in (1, 2, 3):
+        scatter_finish(u)
 
     back_landed(1, dx_out)
     back_sent(1)
@@ -885,17 +1005,17 @@
     pair_sent(3, dyb)
     part_sent(2)
     part_sent(3)
-    for k in range(KINDS):
-        scatter_sent(k)
-
-
-def whole_layer(mesh, tok, cot, packed, gains, codes):
+    for u in range(len(SCATTER)):
+        scatter_sent(u)
+
+
+def whole_layer(mesh, tok, cot, first, up, down, gains, padding, lengths):
     depth = mesh.shape["tensor"]
     bit_count = (mesh.shape["dp"] // 2).bit_length() - 1
     columns = 1 << bit_count
-    shard = packed.shape[1]
+    shard = up.shape[0]
     half = depth // 2
-    rows = codes.shape[1]
+    rows = padding.shape[1]
     own = rows // 2
     vmem = pl.BlockSpec(memory_space=pltpu.VMEM)
     hbm = pl.BlockSpec(memory_space=pl.ANY)
@@ -925,8 +1045,10 @@
         ((half, TILE, D), BF16),
         ((KINDS, 2, columns - 1, half, shard, D), BF16),
         ((KINDS, depth, shard, D), BF16),
-        ((2 * columns, 8, D), F32),
-        ((2,) + codes.shape, F32),
+        ((KINDS, 2, half, shard, D), BF16),
+        ((2 * columns, 8, 128), F32),
+        ((8, D), F32),
+        ((2, 8, rows), F32),
         ((8, D), F32),
         ((2 * depth, 8, D), F32),
         ((columns, 8, D), F32),
@@ -938,17 +1060,17 @@
         "gain_s": (2 * columns,),
         "gain_r": (2 * columns,),
         "code_s": (),
-        "code_l": (),
         "code_r": (),
-        "z_s": (KINDS, depth),
-        "z_r": (KINDS, 2, half),
-        "rel_s": (KINDS, 2),
-        "x_s": (KINDS, 2, bit_count, blocks),
-        "x_r": (KINDS, 2, bit_count, blocks),
-        "rs_s": (KINDS, 2, bit_count, blocks),
-        "rs_r": (KINDS, 2, bit_count, blocks),
-        "rz_s": (KINDS, 2, half),
-        "rz_r": (KINDS, depth),
+        "z_s": (len(GATHER), depth),
+        "z_r": (len(GATHER), 2, half),
+        "rel_s": (len(GATHER), 2, half),
+        "x_s": (len(GATHER), 2, bit_count, blocks),
+        "x_r": (len(GATHER), 2, bit_count, blocks),
+        "rs_s": (len(SCATTER), 2, bit_count, blocks),
+        "rs_r": (len(SCATTER), 2, bit_count, blocks),
+        "rz_s": (len(SCATTER), 2, half),
+        "rz_r": (len(SCATTER), depth),
+        "far_r": (len(SCATTER), 2, half),
         "out_s": (2, half),
         "out_r": (2, 2),
         "pa_s": (4,),
@@ -965,10 +1087,10 @@
         out_shape=(
             jax.ShapeDtypeStruct(tok.shape, BF16),
             jax.ShapeDtypeStruct(tok.shape, BF16),
-            jax.ShapeDtypeStruct(packed.shape, F32),
-            jax.ShapeDtypeStruct((8, D), F32),
+            jax.ShapeDtypeStruct((KINDS,) + up.shape, F32),
+            jax.ShapeDtypeStruct((8, 128), F32),
         ),
-        in_specs=[hbm, hbm, hbm, vmem, vmem],
+        in_specs=[hbm] * 5 + [vmem, vmem, pl.BlockSpec(memory_space=pltpu.SMEM)],
         out_specs=(hbm, hbm, vmem, vmem),
         scratch_shapes=[pltpu.VMEM(shape, dtype) for shape, dtype in scratch]
         + [sem(sems[name]) for name in SEMS],
@@ -976,51 +1098,41 @@
             collective_id=0, has_side_effects=True, vmem_limit_bytes=67043328
         ),
         name="whole_layer",
-    )(tok, cot, packed, gains, codes)
+    )(tok, cot, first, up, down, gains, padding, lengths)
 
 
 def block_body(mesh, tokens, cotangent, lengths, padding, ln_gain, w_qkv, w_out, w_up, w_down):
     depth = mesh.shape["tensor"]
-    dp = lax.axis_index("dp")
-    z = lax.axis_index("tensor")
     shard = w_up.shape[1]
-    width = w_qkv.shape[3]
     pair = 2 * HD
 
     qkv = w_qkv[0]
     out_t = w_out[0].T
-    packed = jnp.stack(
+    packed = jnp.concatenate(
         [
-            jnp.concatenate(
-                [
-                    qkv[:, 0, :pair],
-                    qkv[:, 1, :pair],
-                    qkv[:, 2, :pair],
-                    qkv[:, 0, pair:],
-                    qkv[:, 1, pair:],
-                    qkv[:, 2, pair:],
-                    out_t[:, pair:],
-                    out_t[:, :pair],
-                ],
-                axis=1,
-            ),
-            w_up[0],
-            w_down[0].T,
-        ]
+            qkv[:, 0, :pair],
+            qkv[:, 1, :pair],
+            qkv[:, 2, :pair],
+            qkv[:, 0, pair:],
+            qkv[:, 1, pair:],
+            qkv[:, 2, pair:],
+            out_t[:, pair:],
+            out_t[:, :pair],
+        ],
+        axis=1,
     )
-    gain_rows = jnp.zeros((8, D), F32)
-    gain_rows = lax.dynamic_update_slice(gain_rows, ln_gain[0].astype(F32), (0, dp * shard))
-    places = lax.iota(jnp.int32, padding.shape[1])
-    bounds = jnp.cumsum(lengths[:, 0], axis=1)
-    picture = jnp.sum((places[None, :, None] >= bounds[:, None, :]).astype(jnp.int32), axis=2)
-    key_code = jnp.where(padding == 1, picture, -1)
-    codes = jnp.concatenate([picture, key_code, picture, picture], axis=0).astype(F32)
-
     y_back, dx_back, summed, gain_sum = whole_layer(
-        mesh, tokens, cotangent, packed, gain_rows, codes
+        mesh,
+        tokens,
+        cotangent,
+        packed,
+        w_up[0],
+        w_down[0].T,
+        ln_gain[0],
+        padding,
+        lengths[:, 0],
     )
-    part = 2 * D // (mesh.shape["dp"] * depth)
-    gain_result = lax.dynamic_slice(gain_sum[:2].reshape(-1), ((dp * depth + z) * part,), (part,))
+    gain_result = gain_sum[0, : 2 * D // (mesh.shape["dp"] * depth)]
     first = summed[0]
     qkv_grad = jnp.stack(
         [
@@ -1280,7 +1392,7 @@
         depth == 4
         and dp_size >= 4
         and columns & (columns - 1) == 0
-        and D % (dp_size * 32) == 0
+        and D == dp_size * 2 * HALF
         and tokens.shape[0] == 2
         and tokens.shape[1] == dp_size * depth * TILE
         and w_qkv.shape[0] == 1

time: 220 us -> 183 us (0.83)
  Pallas kernels: 202 us -> 171 us
  other arithmetic: 9.15 us -> 4.4 us
    pallas_call x1, Pallas kernels: 202 us -> 171 us  [whole_layer(): pl.pallas_call(functools.partial(layer_kernel, depth, bit_count, shard, r...]
    another operation x2 -> x0, other arithmetic: 2.65 us -> none  [the longest x1 1.8 us: block_body(): jnp.stack([jnp.concatenate([qkv[:, 0, :pair], qkv[:, 1, :pair], qkv[:, 2,...]
where the time goes in v3:
time: 183 us
  Pallas kernels  171 us (93%)
  local copies, waits for them, and re-layouts  6.2 us (3%)
  other arithmetic  4.4 us (2%)
    pallas_call x1, Pallas kernels, whole_layer(): pl.pallas_call(functools.partial(layer_kernel, depth, bit_count, shard, r...  171 us

profile of v3, /device:TPU:1, one launch (start us, length us, event | category | flops | bytes accessed | tf_op | source)
XLA Modules:
  0.0 182.6 jit_solution(15587557985983957576)
XLA Ops:
  0.6 0.9 copy.16
  1.6 0.8 slice_bitcast_fusion.2
  2.3 0.8 slice_bitcast_fusion.5
  3.1 0.8 concatenate.15.refs_2_
  3.9 171.3 %whole_layer.1 = (bf16[2,256,768]{2,1,0:T(8,128)(2,1)}, bf16[2,256,768]{2,1,0:T(8,128)(2,1)}, f32[3,96,768]{2,1,0:T(8,128)}, f32[8,128]{1,0:T(8,128)}) custom-call(bf16[2,256,768]{2,1,0:T(8,128)(2,1)} %refs_0_.1, bf16[2,256,768]{2,1,0:T(8,128)(2,1)} %refs_1_.1, bf16[96,768]{1,0:T(8,128)(2,1)} %concatenate.15.refs_2_, bf16[96,768]{1,0:T(8,128)(2,1)} %bitcast.46, ...), custom_call_target="tpu_custom_call" | custom-call | tf_op jit(solution)/shard_map/whole_layer/pallas_call | solution.py:1085
  175.2 0.0 copy-start
  175.2 1.3 slice_bitcast_fusion.8
  176.5 2.4 %convert_element_type.6 = f32[2,256,768]{2,1,0:T(8,128)} convert(bf16[2,256,768]{2,1,0:T(8,128)(2,1)} %get-tuple-element.11) | non-fusion elementwise | flops 393216 | bytes 2359296 | tf_op jit(solution)/shard_map/convert_element_type | solution.py:1152
  178.8 0.0 copy-done
  178.8 0.9 slice_bitcast_fusion
  179.7 0.0 copy-start.1
  179.7 0.1 fusion.1
  179.9 0.7 copy.17
  180.6 0.7 maximum_bitcast_fusion
  181.3 0.0 copy-done.1
  181.4 1.3 convert_element_type.7
  (5 shorter events, 0.1 us)
Async XLA Ops:
  175.2 3.7 %copy-start = (f32[3,96,768]{2,1,0:T(8,128)S(1)}, f32[3,96,768]{2,1,0:T(8,128)}, u32[]{:S(2)}) copy-start(f32[3,96,768]{2,1,0:T(8,128)} %get-tuple-element.14) | copy-start | bytes 2654212
  179.7 1.6 copy-start.1

commit v4 on v3

--- a/solution.py
+++ b/solution.py
@@ -151,8 +151,9 @@
         sum_rx,
         all_rx,
         delta,
-    ) = refs[12:43]
-    sem = dict(zip(SEMS, refs[43:]))
+        shares,
+    ) = refs[12:44]
+    sem = dict(zip(SEMS, refs[44:]))
     half = depth // 2
     columns = 1 << bit_count
     own_rows = rows // 2
@@ -354,7 +355,7 @@
         unit = GATHER[u]
         return wts.at[unit[0], slot, unit_rows(unit, p, color)]
 
-    def after_z(u):
+    def gather_z_landed(u):
         unit = GATHER[u]
         for color in range(2):
             for slot in range(half):
@@ -362,8 +363,10 @@
                     wts.at[unit[0], slot, unit_rows(unit, p, color)], sem["z_r"].at[u, color, slot]
                 )
 
+    def forward(u):
         @pl.when(relays)
         def _():
+            gather_z_landed(u)
             for color in range(2):
                 for slot in range(half):
                     block = relay_block(u, color, slot)
@@ -375,6 +378,8 @@
                         relay_to,
                     ).start()
 
+    def after_z(u):
+        pl.when(jnp.logical_not(relays))(functools.partial(gather_z_landed, u))
         gather_step(u, 0)
 
     def gather_blocks(u, color, s, landed):
@@ -612,10 +617,12 @@
         qtz[h, HD * (1 - h % 2) : HD * (1 - h % 2) + HD, :] = jnp.zeros((HD, rows), BF16)
     gsum[...] = jnp.zeros(gsum.shape, F32)
     clear_far()
+    forward(0)
     after_z(0)
     finish_small()
     gain_first = gains[0:1, :]
     gain_second = gains[1:2, :]
+    forward(1)
     after_z(1)
     gather_next(0, 0)
 
@@ -630,15 +637,16 @@
         row_id = lax.broadcasted_iota(jnp.int32, (128, rows), 0) + 128 * block
         col_id = lax.broadcasted_iota(jnp.int32, (128, rows), 1)
         seen = jnp.logical_or(key == query_image, row_id == col_id)
-        bias[span, :] = jnp.where(seen, 0.0, NEGATIVE).astype(BF16)
-
+        bias[span, :] = jnp.where(seen, 0.0, NEGATIVE)
+
+    forward(2)
     after_z(2)
     gather_next(1, 0)
+    forward(3)
     after_z(3)
     gather_z(4)
     gather_next(2, 0)
     rows_landed(0)
-    send_rows(1, cot)
 
     def first_norm(i, at, base):
         normed, _ = normalize(xb[i].astype(F32))
@@ -683,19 +691,23 @@
                 vt[:, span] = turned
 
     each_half(project, lambda: pair_landed(0, ab))
+    forward(4)
+    send_rows(1, cot)
 
     def attend(base, hook):
         span = pl.ds(base, own_rows)
         for h in range(6):
             pair = h // 2
             keys = qkv[:, 384 + 128 * pair : 512 + 128 * pair]
-            scores = dot(keys, qtz[h, :, span]) + bias[:, span].astype(F32)
+            scores = dot(keys, qtz[h, :, span]) + bias[:, span]
             highest = jnp.max(scores, axis=0, keepdims=True)
             exponent = jnp.exp(scores - highest)
             total = jnp.sum(exponent, axis=0, keepdims=True)
-            rounded = (exponent * (1.0 / total)).astype(BF16)
+            rounded = exponent.astype(BF16)
             pt[h, :, span] = rounded
-            mixed = dot(vt[HD * h : HD * h + HD, :], rounded)
+            share = 1.0 / total
+            shares[h, :, span] = share
+            mixed = dot(vt[HD * h : HD * h + HD, :], rounded) * share
             ott[HD * h : HD * h + HD, span] = mixed.astype(BF16)
             hook(h)
         orow[span, :] = ott[:, span].T
@@ -723,12 +735,15 @@
                     gather_next(4, 0)
 
         attend(base, hook)
+
+        @pl.when(i == 0)
+        def _():
+            prs[0] = dot_nt(orow[pl.ds(base, own_rows), :], wq[:, 1152:1536]).astype(BF16)
+            part_send(0)
+
         return carry
 
     lax.fori_loop(0, 2, attend_loop, 0)
-    out_weight = wq[:, 1152:1536]
-    prs[0] = dot_nt(orow[pl.ds(theirs, own_rows), :], out_weight).astype(BF16)
-    part_send(0)
 
     def own_out(i, at, base):
         mid[pl.ds(at, TILE), :] = dot_nt(orow[pl.ds(base, TILE), :], wq[:, 1152:1536])
@@ -821,6 +836,7 @@
     each_half(through_gelu)
     part_sent(0)
     their_chunks(dgel, 1, prs.at[0])
+    part_send(2)
     part_landed(1)
 
     def layer_rows(i, at, base):
@@ -829,7 +845,6 @@
         stage[i] = (mid[here, :] + total).astype(BF16)
 
     own_chunks(layer_rows)
-    part_send(2)
     send_back(0, y_out)
     pair_sent(2, dyb)
     part_landed(2)
@@ -855,14 +870,17 @@
     def spread_mix(base):
         span = pl.ds(base, own_rows)
         result = dot(dyb[span, :], wq[:, 1152:1536])
-        dorow[span, :] = result.astype(BF16)
-        turned = result.T.astype(BF16)
+        result = result.astype(BF16).astype(F32)
+        turned = result.T
+        pieces = []
         for h in range(6):
             at = HD * (h % 2)
-            piece = turned[HD * h : HD * h + HD]
+            piece = (turned[HD * h : HD * h + HD] * shares[h, :, span]).astype(BF16)
+            pieces.append(piece.astype(F32))
             qtz[h, at : at + HD, span] = piece
             product = piece.astype(F32) * ott[HD * h : HD * h + HD, span].astype(F32)
             delta[h, :, span] = jnp.sum(product, axis=0, keepdims=True)
+        dorow[span, :] = jnp.concatenate(pieces, axis=0).T.astype(BF16)
 
     each_half(spread_mix, lambda: pair_landed(3, dyb))
 
@@ -1033,7 +1051,7 @@
         ((384, rows), BF16),
         ((384, rows), BF16),
         ((6, rows, rows), BF16),
-        ((rows, rows), BF16),
+        ((rows, rows), F32),
         ((384, rows), BF16),
         ((rows, 384), BF16),
         ((rows, 384), BF16),
@@ -1052,6 +1070,7 @@
         ((8, D), F32),
         ((2 * depth, 8, D), F32),
         ((columns, 8, D), F32),
+        ((6, 1, rows), F32),
         ((6, 1, rows), F32),
     ]
     sems = {

time: 183 us -> 178 us (0.973)
  Pallas kernels: 171 us -> 166 us
    pallas_call x1, Pallas kernels: 171 us -> 166 us  [whole_layer(): pl.pallas_call(functools.partial(layer_kernel, depth, bit_count, shard, r...]
where the time goes in v4:
time: 178 us
  Pallas kernels  166 us (93%)
  local copies, waits for them, and re-layouts  6.2 us (3%)
  other arithmetic  4.4 us (2%)
    pallas_call x1, Pallas kernels, whole_layer(): pl.pallas_call(functools.partial(layer_kernel, depth, bit_count, shard, r...  166 us

profile of v4, /device:TPU:1, one launch (start us, length us, event | category | flops | bytes accessed | tf_op | source)
XLA Modules:
  0.0 177.8 jit_solution(17107290523143669766)
XLA Ops:
  0.6 0.9 copy.16
  1.6 0.8 slice_bitcast_fusion.2
  2.3 0.8 slice_bitcast_fusion.5
  3.1 0.8 concatenate.15.refs_2_
  3.9 166.5 %whole_layer.1 = (bf16[2,256,768]{2,1,0:T(8,128)(2,1)}, bf16[2,256,768]{2,1,0:T(8,128)(2,1)}, f32[3,96,768]{2,1,0:T(8,128)}, f32[8,128]{1,0:T(8,128)}) custom-call(bf16[2,256,768]{2,1,0:T(8,128)(2,1)} %refs_0_.1, bf16[2,256,768]{2,1,0:T(8,128)(2,1)} %refs_1_.1, bf16[96,768]{1,0:T(8,128)(2,1)} %concatenate.15.refs_2_, bf16[96,768]{1,0:T(8,128)(2,1)} %bitcast.46, ...), custom_call_target="tpu_custom_call" | custom-call | tf_op jit(solution)/shard_map/whole_layer/pallas_call | solution.py:1104
  170.4 0.0 copy-start
  170.4 1.3 slice_bitcast_fusion.8
  171.6 2.4 %convert_element_type.6 = f32[2,256,768]{2,1,0:T(8,128)} convert(bf16[2,256,768]{2,1,0:T(8,128)(2,1)} %get-tuple-element.11) | non-fusion elementwise | flops 393216 | bytes 2359296 | tf_op jit(solution)/shard_map/convert_element_type | solution.py:1171
  174.0 0.0 copy-done
  174.0 0.9 slice_bitcast_fusion
  174.9 0.0 copy-start.1
  174.9 0.1 fusion.1
  175.0 0.7 copy.17
  175.8 0.7 maximum_bitcast_fusion
  176.5 0.0 copy-done.1
  176.5 1.3 convert_element_type.7
  (5 shorter events, 0.1 us)
Async XLA Ops:
  170.4 3.7 %copy-start = (f32[3,96,768]{2,1,0:T(8,128)S(1)}, f32[3,96,768]{2,1,0:T(8,128)}, u32[]{:S(2)}) copy-start(f32[3,96,768]{2,1,0:T(8,128)} %get-tuple-element.14) | copy-start | bytes 2654212
  174.9 1.6 copy-start.1

commit v5 on v4

--- a/solution.py
+++ b/solution.py
@@ -16,8 +16,22 @@
 BF16 = jnp.bfloat16
 KINDS = 3
 HALF = 48
-GATHER = ((0, 0, HALF), (0, HALF, HALF), (1, 0, HALF), (1, HALF, HALF), (2, 0, 2 * HALF))
-SCATTER = ((2, 0, 2 * HALF), (1, 0, 2 * HALF), (0, 0, HALF), (0, HALF, HALF))
+GATHER = (
+    (0, 0, 16),
+    (0, 16, 32),
+    (0, HALF, HALF),
+    (1, 0, HALF),
+    (1, HALF, HALF),
+    (2, 0, 2 * HALF),
+)
+SCATTER = (
+    (2, 0, HALF),
+    (2, HALF, HALF),
+    (1, 0, HALF),
+    (1, HALF, HALF),
+    (0, 0, HALF),
+    (0, HALF, HALF),
+)
 RELAYED = (2, 1, 0)
 TILE = 256
 SCALE = HD**-0.5
@@ -609,7 +623,7 @@
     make_small()
     entry_barrier()
     send_small()
-    for u in range(4):
+    for u in range(5):
         gather_z(u)
     send_rows(0, tok)
 
@@ -626,6 +640,15 @@
     after_z(1)
     gather_next(0, 0)
 
+    forward(2)
+    after_z(2)
+    gather_next(1, 0)
+    forward(3)
+    after_z(3)
+    gather_next(2, 0)
+    forward(4)
+    after_z(4)
+    gather_z(5)
     micro = z // 2
     owner = z % 2
     query_image = code[owner, pl.ds(micro, 1), :]
@@ -639,13 +662,7 @@
         seen = jnp.logical_or(key == query_image, row_id == col_id)
         bias[span, :] = jnp.where(seen, 0.0, NEGATIVE)
 
-    forward(2)
-    after_z(2)
-    gather_next(1, 0)
-    forward(3)
-    after_z(3)
-    gather_z(4)
-    gather_next(2, 0)
+    gather_next(3, 0)
     rows_landed(0)
 
     def first_norm(i, at, base):
@@ -654,7 +671,7 @@
 
     own_chunks(first_norm)
     pair_send(0, ab)
-    gather_last(0, 1)
+    gather_last(0, 1, 2)
 
     def roll(value):
         return pltpu.roll(value, HD, 1)
@@ -690,9 +707,8 @@
             else:
                 vt[:, span] = turned
 
+    forward(5)
     each_half(project, lambda: pair_landed(0, ab))
-    forward(4)
-    send_rows(1, cot)
 
     def attend(base, hook):
         span = pl.ds(base, own_rows)
@@ -716,23 +732,29 @@
         base = pl.multiple_of(jnp.where(i == 0, theirs, mine), own_rows)
 
         def hook(h):
+            if h == 0:
+
+                @pl.when(i == 1)
+                def _():
+                    send_rows(1, cot)
+
             if h == 1:
 
                 @pl.when(i == 0)
                 def _():
-                    gather_next(3, 0)
+                    gather_next(4, 0)
 
             if h == 4:
 
                 @pl.when(i == 0)
                 def _():
-                    after_z(4)
+                    after_z(5)
 
             if h == 5:
 
                 @pl.when(i == 1)
                 def _():
-                    gather_next(4, 0)
+                    gather_next(5, 0)
 
         attend(base, hook)
 
@@ -760,7 +782,7 @@
 
     own_chunks(second_norm)
     pair_send(1, bnb)
-    gather_last(2, 3)
+    gather_last(3, 4)
 
     def expand(base):
         def chunk(i, carry):
@@ -801,7 +823,8 @@
     pair_landed(2, dyb)
     grad_tiles(dyb, place[2], down_tile)
     scatter_step(0, 0)
-    gather_last(4)
+    scatter_step(1, 0)
+    gather_last(5)
 
     def contract(base, j_refs, weight):
         total = dot_nt(j_refs[0, pl.ds(base, TILE), :], wts[weight, 0])
@@ -845,6 +868,7 @@
         stage[i] = (mid[here, :] + total).astype(BF16)
 
     own_chunks(layer_rows)
+    scatter_next(0, 0)
     send_back(0, y_out)
     pair_sent(2, dyb)
     part_landed(2)
@@ -863,9 +887,10 @@
     own_chunks(second_back)
     pair_send(3, dyb)
     gather_sent(1)
-    scatter_next(0, 0)
+    scatter_next(1, 0)
     grad_tiles(bnb, place[1], up_tile)
-    scatter_step(1, 0)
+    scatter_step(2, 0)
+    scatter_step(3, 0)
 
     def spread_mix(base):
         span = pl.ds(base, own_rows)
@@ -883,6 +908,7 @@
         dorow[span, :] = jnp.concatenate(pieces, axis=0).T.astype(BF16)
 
     each_half(spread_mix, lambda: pair_landed(3, dyb))
+    scatter_last(0)
 
     def attend_back(pair, carry):
         def tile(offset):
@@ -908,11 +934,15 @@
 
         @pl.when(pair == 0)
         def _():
-            scatter_last(0)
+            scatter_last(1)
+
+        @pl.when(pair == 1)
+        def _():
+            scatter_next(2, 0)
 
         @pl.when(pair == 2)
         def _():
-            scatter_next(1, 0)
+            scatter_next(3, 0)
 
         return carry
 
@@ -949,13 +979,14 @@
         return carry
 
     lax.fori_loop(0, D // TILE, first_tiles, 0)
-    scatter_step(2, 0)
-    scatter_step(3, 0)
+    scatter_step(4, 0)
+    scatter_step(5, 0)
 
     back_sent(0)
     back_landed(0, y_out)
     scatter_relay(0)
-    scatter_last(1)
+    scatter_last(2)
+    scatter_relay(1)
     part_landed(3)
 
     def first_back(i, at, base):
@@ -978,12 +1009,14 @@
             device(p, cc, zz),
         ).start()
     pltpu.make_async_copy(gsum, sum_rx.at[me], sem["sum_r"].at[me]).start()
+    scatter_last(3)
     send_back(1, dx_out)
-    scatter_next(2, 0)
-    scatter_next(3, 0)
-    scatter_relay(1)
-    scatter_last(2)
-    scatter_last(3)
+    scatter_next(4, 0)
+    scatter_relay(2)
+    scatter_next(5, 0)
+    scatter_relay(3)
+    scatter_last(4)
+    scatter_last(5)
     for source in range(2 * depth):
         wait_bytes(sum_rx.at[source], sem["sum_r"].at[source])
     for index in range(len(column_peers)):
@@ -997,9 +1030,10 @@
             gsum, all_rx.at[p], sem["all_s"].at[index], sem["all_r"].at[p], device(pp, c, z)
         ).start()
     pltpu.make_async_copy(gsum, all_rx.at[p], sem["all_r"].at[p]).start()
-    scatter_relay(2)
-    scatter_relay(3)
+    scatter_relay(4)
+    scatter_relay(5)
     scatter_finish(0)
+    scatter_finish(1)
     for source in range(columns):
         wait_bytes(all_rx.at[source], sem["all_r"].at[source])
     for index in range(len(plane_peers)):
@@ -1011,7 +1045,7 @@
     wanted = jnp.where(place_of < D, total[0:1, :], total[1:2, :])
     turn = (D - place_of % D) % D
     gm_out[...] = pltpu.roll(jnp.broadcast_to(wanted, (8, D)), turn, 1)[:, 0:128]
-    for u in (1, 2, 3):
+    for u in (2, 3, 4, 5):
         scatter_finish(u)
 
     back_landed(1, dx_out)

time: 178 us -> 172 us (0.966)
  Pallas kernels: 166 us -> 160 us
    pallas_call x1, Pallas kernels: 166 us -> 160 us  [whole_layer(): pl.pallas_call(functools.partial(layer_kernel, depth, bit_count, shard, r...]
where the time goes in v5:
time: 172 us; the launch traced here: 171 us
  Pallas kernels  160 us (93%)
  local copies, waits for them, and re-layouts  6.2 us (4%)
  other arithmetic  4.4 us (3%)
    pallas_call x1, Pallas kernels, whole_layer(): pl.pallas_call(functools.partial(layer_kernel, depth, bit_count, shard, r...  160 us

profile of v5, /device:TPU:1, one launch (start us, length us, event | category | flops | bytes accessed | tf_op | source)
XLA Modules:
  0.0 171.4 jit_solution(11834108335688800067)
XLA Ops:
  0.6 0.9 copy.16
  1.6 0.8 slice_bitcast_fusion.2
  2.3 0.8 slice_bitcast_fusion.5
  3.1 0.8 concatenate.15.refs_2_
  3.9 160.0 %whole_layer.1 = (bf16[2,256,768]{2,1,0:T(8,128)(2,1)}, bf16[2,256,768]{2,1,0:T(8,128)(2,1)}, f32[3,96,768]{2,1,0:T(8,128)}, f32[8,128]{1,0:T(8,128)}) custom-call(bf16[2,256,768]{2,1,0:T(8,128)(2,1)} %refs_0_.1, bf16[2,256,768]{2,1,0:T(8,128)(2,1)} %refs_1_.1, bf16[96,768]{1,0:T(8,128)(2,1)} %concatenate.15.refs_2_, bf16[96,768]{1,0:T(8,128)(2,1)} %bitcast.46, ...), custom_call_target="tpu_custom_call" | custom-call | tf_op jit(solution)/shard_map/whole_layer/pallas_call | solution.py:1138
  163.9 0.0 copy-start
  163.9 1.3 slice_bitcast_fusion.8
  165.2 2.4 %convert_element_type.6 = f32[2,256,768]{2,1,0:T(8,128)} convert(bf16[2,256,768]{2,1,0:T(8,128)(2,1)} %get-tuple-element.11) | non-fusion elementwise | flops 393216 | bytes 2359296 | tf_op jit(solution)/shard_map/convert_element_type | solution.py:1205
  167.6 0.0 copy-done
  167.6 0.9 slice_bitcast_fusion
  168.5 0.0 copy-start.1
  168.5 0.1 fusion.1
  168.6 0.7 copy.17
  169.4 0.7 maximum_bitcast_fusion
  170.1 0.0 copy-done.1
  170.1 1.3 convert_element_type.7
  (5 shorter events, 0.1 us)
Async XLA Ops:
  163.9 3.7 %copy-start = (f32[3,96,768]{2,1,0:T(8,128)S(1)}, f32[3,96,768]{2,1,0:T(8,128)}, u32[]{:S(2)}) copy-start(f32[3,96,768]{2,1,0:T(8,128)} %get-tuple-element.14) | copy-start | bytes 2654212
  168.5 1.6 copy-start.1

commit v6 on v5

--- a/solution.py
+++ b/solution.py
@@ -277,8 +277,8 @@
             return xb.at[slot]
         return dyb.at[pl.ds(pl.multiple_of(own_rows * to_c + TILE * slot, TILE), TILE)]
 
-    def send_rows(which, array):
-        for m, to_c, to_z, is_self in row_targets():
+    def send_rows(which, array, to_ends=None):
+        def send(m, to_c, to_z, is_self):
             slot = z % half
             send_or_copy(
                 is_self,
@@ -288,6 +288,13 @@
                 sem["tok_r"].at[which, slot],
                 device(p, to_c, to_z),
             )
+
+        for m, to_c, to_z, is_self in row_targets():
+            ship = functools.partial(send, m, to_c, to_z, is_self)
+            if to_ends is None:
+                ship()
+            else:
+                pl.when((c == m) if to_ends else (c != m))(ship)
 
     def rows_sent(which, array):
         for m, to_c, to_z, is_self in row_targets():
@@ -736,13 +743,14 @@
 
                 @pl.when(i == 1)
                 def _():
-                    send_rows(1, cot)
+                    send_rows(1, cot, True)
 
             if h == 1:
 
                 @pl.when(i == 0)
                 def _():
                     gather_next(4, 0)
+                    send_rows(1, cot, False)
 
             if h == 4:
 

time: 172 us -> 171 us (level)
  no operation moved by 1% of the time
where the time goes in v6:
time: 171 us; the launch traced here: 170 us
  Pallas kernels  159 us (93%)
  local copies, waits for them, and re-layouts  6.2 us (4%)
  other arithmetic  4.4 us (3%)
    pallas_call x1, Pallas kernels, whole_layer(): pl.pallas_call(functools.partial(layer_kernel, depth, bit_count, shard, r...  159 us

profile of v6, /device:TPU:1, one launch (start us, length us, event | category | flops | bytes accessed | tf_op | source)
XLA Modules:
  0.0 170.5 jit_solution(4536160519789747228)
XLA Ops:
  0.6 0.9 copy.16
  1.6 0.8 slice_bitcast_fusion.2
  2.3 0.8 slice_bitcast_fusion.5
  3.1 0.8 concatenate.15.refs_2_
  3.9 159.2 %whole_layer.1 = (bf16[2,256,768]{2,1,0:T(8,128)(2,1)}, bf16[2,256,768]{2,1,0:T(8,128)(2,1)}, f32[3,96,768]{2,1,0:T(8,128)}, f32[8,128]{1,0:T(8,128)}) custom-call(bf16[2,256,768]{2,1,0:T(8,128)(2,1)} %refs_0_.1, bf16[2,256,768]{2,1,0:T(8,128)(2,1)} %refs_1_.1, bf16[96,768]{1,0:T(8,128)(2,1)} %concatenate.15.refs_2_, bf16[96,768]{1,0:T(8,128)(2,1)} %bitcast.46, ...), custom_call_target="tpu_custom_call" | custom-call | tf_op jit(solution)/shard_map/whole_layer/pallas_call | solution.py:1146
  163.1 0.0 copy-start
  163.1 1.3 slice_bitcast_fusion.8
  164.3 2.4 %convert_element_type.6 = f32[2,256,768]{2,1,0:T(8,128)} convert(bf16[2,256,768]{2,1,0:T(8,128)(2,1)} %get-tuple-element.11) | non-fusion elementwise | flops 393216 | bytes 2359296 | tf_op jit(solution)/shard_map/convert_element_type | solution.py:1213
  166.7 0.0 copy-done
  166.7 0.9 slice_bitcast_fusion
  167.6 0.0 copy-start.1
  167.6 0.1 fusion.1
  167.7 0.7 copy.17
  168.5 0.7 maximum_bitcast_fusion
  169.2 0.0 copy-done.1
  169.2 1.3 convert_element_type.7
  (5 shorter events, 0.1 us)
Async XLA Ops:
  163.1 3.7 %copy-start = (f32[3,96,768]{2,1,0:T(8,128)S(1)}, f32[3,96,768]{2,1,0:T(8,128)}, u32[]{:S(2)}) copy-start(f32[3,96,768]{2,1,0:T(8,128)} %get-tuple-element.14) | copy-start | bytes 2654212
  167.6 1.6 copy-start.1

commit v7 on v6

--- a/solution.py
+++ b/solution.py
@@ -132,7 +132,8 @@
 
 def layer_kernel(depth, bit_count, shard, rows, *refs):
     (tok, cot, first_in, up_in, down_in, gain_in, pad_in, length_in) = refs[:8]
-    (y_out, dx_out, g_out, gm_out) = refs[8:12]
+    (rows_out, g_out, gm_out) = refs[8:11]
+    y_out, dx_out = rows_out.at[0], rows_out.at[1]
     (
         xb,
         dyb,
@@ -166,8 +167,8 @@
         all_rx,
         delta,
         shares,
-    ) = refs[12:44]
-    sem = dict(zip(SEMS, refs[44:]))
+    ) = refs[11:43]
+    sem = dict(zip(SEMS, refs[43:]))
     half = depth // 2
     columns = 1 << bit_count
     own_rows = rows // 2
@@ -1146,13 +1147,12 @@
     return pl.pallas_call(
         functools.partial(layer_kernel, depth, bit_count, shard, rows),
         out_shape=(
-            jax.ShapeDtypeStruct(tok.shape, BF16),
-            jax.ShapeDtypeStruct(tok.shape, BF16),
+            jax.ShapeDtypeStruct((2,) + tok.shape, BF16),
             jax.ShapeDtypeStruct((KINDS,) + up.shape, F32),
             jax.ShapeDtypeStruct((8, 128), F32),
         ),
         in_specs=[hbm] * 5 + [vmem, vmem, pl.BlockSpec(memory_space=pltpu.SMEM)],
-        out_specs=(hbm, hbm, vmem, vmem),
+        out_specs=(hbm, vmem, vmem),
         scratch_shapes=[pltpu.VMEM(shape, dtype) for shape, dtype in scratch]
         + [sem(sems[name]) for name in SEMS],
         compiler_params=pltpu.CompilerParams(
@@ -1182,7 +1182,7 @@
         ],
         axis=1,
     )
-    y_back, dx_back, summed, gain_sum = whole_layer(
+    rows_back, summed, gain_sum = whole_layer(
         mesh,
         tokens,
         cotangent,
@@ -1210,8 +1210,8 @@
     )[None]
     out_grad = jnp.concatenate([first[:, 5 * pair :], first[:, 4 * pair + HD : 5 * pair]], axis=1)
     return (
-        y_back.astype(F32),
-        dx_back.astype(F32),
+        rows_back[0].astype(F32),
+        rows_back[1].astype(F32),
         gain_result,
         qkv_grad,
         out_grad.T[None],

time: 171 us -> 171 us (level)
    convert_element_type x2 -> x1, other arithmetic: 3.64 us -> 3.37 us  [block_body(): rows_back[1].astype(F32)]
where the time goes in v7:
time: 171 us; the launch traced here: 170 us
  Pallas kernels  159 us (93%)
  local copies, waits for them, and re-layouts  6.12 us (4%)
  other arithmetic  4.14 us (2%)
    pallas_call x1, Pallas kernels, whole_layer(): pl.pallas_call(functools.partial(layer_kernel, depth, bit_count, shard, r...  159 us

profile of v7, /device:TPU:1, one launch (start us, length us, event | category | flops | bytes accessed | tf_op | source)
XLA Modules:
  0.0 170.1 jit_solution(1903741184227518504)
XLA Ops:
  0.6 0.8 slice_bitcast_fusion.5
  1.4 0.8 slice_bitcast_fusion.2
  2.2 0.9 copy.16
  3.1 0.8 concatenate.15.refs_2_
  3.9 159.2 %whole_layer.1 = (bf16[2,2,256,768]{3,2,1,0:T(8,128)(2,1)}, f32[3,96,768]{2,1,0:T(8,128)}, f32[8,128]{1,0:T(8,128)}) custom-call(bf16[2,256,768]{2,1,0:T(8,128)(2,1)} %refs_0_.1, bf16[2,256,768]{2,1,0:T(8,128)(2,1)} %refs_1_.1, bf16[96,768]{1,0:T(8,128)(2,1)} %concatenate.15.refs_2_, bf16[96,768]{1,0:T(8,128)(2,1)} %bitcast.52, bf16[96,768]{1,0:T(8,128)(2,1)} %bitcast.53, ...), custom_call_target="tpu_custom_call" | custom-call | tf_op jit(solution)/shard_map/whole_layer/pallas_call | solution.py:1147
  163.1 0.0 copy-start
  163.1 3.4 %bitcast_convert_fusion = (f32[2,256,768]{2,1,0:T(8,128)}, f32[2,256,768]{2,1,0:T(8,128)}) fusion(bf16[2,2,256,768]{3,2,1,0:T(8,128)(2,1)} %get-tuple-element.10), kind=kLoop, calls=%fused_computation | loop fusion | flops 786432 | bytes 4718592 | tf_op jit(solution)/shard_map/convert_element_type | solution.py:1214
  166.5 1.2 slice_bitcast_fusion.8
  167.6 0.0 copy-done
  167.6 0.9 slice_bitcast_fusion
  168.5 0.1 fusion.1
  168.7 0.7 maximum_bitcast_fusion
  169.4 0.7 copy.17
  (5 shorter events, 0.1 us)
Async XLA Ops:
  163.1 4.6 %copy-start = (f32[3,96,768]{2,1,0:T(8,128)S(1)}, f32[3,96,768]{2,1,0:T(8,128)}, u32[]{:S(2)}) copy-start(f32[3,96,768]{2,1,0:T(8,128)} %get-tuple-element.12) | copy-start | bytes 2654212
